TPU v7x, 256 devices: a whole 4x4x8 slice. The times are simulated.
256 devices in a mesh: mesh: 32 (over x_lo, z, core), modes: 8 (over x_hi, y).
Axes of the slice: x: 4 (x_hi: 2, x_lo: 2; x = x_hi * 2 + x_lo), y: 4, z: 8, core: 2. Of those that a mesh axis runs over, the one named last changes fastest.
Arguments:
- subspace: float32 [64, 3, 32, 9216], P('modes', None, 'mesh'), may hold values from -14 to 14
- classes: int32 [32, 9216], P('mesh'), may hold values from 0 to 15
- level_density: float32 [16], replicated, may hold values from 0.05 to 1
Outputs:
- residual: float32 [64, 3, 32, 9216], P('modes', None, 'mesh')
- ritz_matrix: float32 [64, 64], replicated
All inputs are finite; a program needn't handle non-finite values.
Results may differ from a plain program's by a relative error of at most 0.0003.
Values sent between devices are 32-bit elements; how exact they have to be, the bound alone decides.
No kernel may reach another device: no remote copies, remote signals or barrier semaphores. Data moves between devices by JAX's collectives and lax.ppermute only.
A program may use at most 128 MiB of HBM per device.

v0:
```python
import functools

import jax
import jax.numpy as jnp
import numpy as np
from jax import lax
from jax.experimental import pallas as pl
from jax.experimental.pallas import tpu as pltpu
from jax.sharding import Mesh
from jax.sharding import PartitionSpec as P

NX = 96
NY = 96
LANES = 128
MODES = ("modes_0", "modes_1")
MESH = ("mesh_0", "mesh_1", "mesh_2")

highest = lax.Precision.HIGHEST
floor_modulus = 0.001
VMEM = pl.BlockSpec(memory_space=pltpu.VMEM)
SMEM = pl.BlockSpec(memory_space=pltpu.SMEM)


def shifted(x, axis, by):
    size = lax.axis_size(axis)
    pairs = [(i, i + by) for i in range(size) if 0 <= i + by < size]
    return lax.ppermute(x, axis, pairs)


def element_matrix():
    poisson_ratio = 0.3
    lame_first = poisson_ratio / ((1 + poisson_ratio) * (1 - 2 * poisson_ratio))
    shear_modulus = 1.0 / (2 * (1 + poisson_ratio))
    elastic = np.zeros((6, 6))
    elastic[:3, :3] = lame_first
    for normal_index in range(3):
        elastic[normal_index, normal_index] = lame_first + 2 * shear_modulus
        elastic[normal_index + 3, normal_index + 3] = shear_modulus
    corner_signs = [
        (1 - 2 * (corner & 1), 1 - 2 * (corner >> 1 & 1), 1 - 2 * (corner >> 2))
        for corner in range(8)
    ]
    gauss_point = 1.0 / np.sqrt(3.0)
    matrix = np.zeros((24, 24))
    for gauss_x in (-gauss_point, gauss_point):
        for gauss_y in (-gauss_point, gauss_point):
            for gauss_z in (-gauss_point, gauss_point):
                strain = np.zeros((6, 24))
                for corner in range(8):
                    sign_x, sign_y, sign_z = corner_signs[corner]
                    deriv_x = 2 * sign_x * (1 + sign_y * gauss_y) * (1 + sign_z * gauss_z) / 8
                    deriv_y = 2 * sign_y * (1 + sign_x * gauss_x) * (1 + sign_z * gauss_z) / 8
                    deriv_z = 2 * sign_z * (1 + sign_x * gauss_x) * (1 + sign_y * gauss_y) / 8
                    column = 3 * corner
                    strain[0, column] = deriv_x
                    strain[1, column + 1] = deriv_y
                    strain[2, column + 2] = deriv_z
                    strain[3, column] = deriv_y
                    strain[3, column + 1] = deriv_x
                    strain[4, column + 1] = deriv_z
                    strain[4, column + 2] = deriv_y
                    strain[5, column] = deriv_z
                    strain[5, column + 2] = deriv_x
                matrix = matrix + strain.T @ elastic @ strain / 8
    return matrix.reshape(8, 3, 8, 3)


def parity_coefficients():
    signs = np.array([[(-1.0) ** bin(p & n).count("1") for n in range(8)] for p in range(8)])
    block = np.einsum("qn,ncmd,pm->qcpd", signs, element_matrix(), signs) / 64
    return tuple(
        float(np.float32(v))
        for v in (
            block[1, 0, 2, 1],
            block[1, 0, 1, 0] - block[1, 0, 2, 1],
            block[1, 1, 1, 1],
            block[3, 0, 3, 0],
            block[3, 0, 6, 2],
            block[3, 2, 5, 1],
            block[7, 0, 7, 0],
        )
    )


LAME, NORMAL, SHEAR, BEND, CROSS, TWIST, LAST = parity_coefficients()


def lane_index(rows):
    return lax.broadcasted_iota(jnp.int32, (rows, LANES), 1)


def rows_of_chunks(v0, v1, v2, lane):
    rows = (
        v0,
        jnp.where(lane < 32, pltpu.roll(v0, 32, 1), pltpu.roll(v1, 32, 1)),
        jnp.where(lane < 64, pltpu.roll(v1, 64, 1), pltpu.roll(v2, 64, 1)),
        pltpu.roll(v2, 96, 1),
    )
    return [jnp.where(lane < NX, r, 0.0) for r in rows]


def chunks_of_rows(o0, o1, o2, o3, lane):
    r1, r2, r3 = pltpu.roll(o1, 96, 1), pltpu.roll(o2, 64, 1), pltpu.roll(o3, 32, 1)
    return (
        jnp.where(lane < 96, o0, r1),
        jnp.where(lane < 64, r1, r2),
        jnp.where(lane < 32, r2, r3),
    )


def prep_kernel(x_ref, classes_ref, levels_ref, pieces_ref, density_ref, modulus_ref):
    classes = classes_ref[...]
    density = jnp.zeros(classes.shape, jnp.float32)
    for level in range(16):
        density = jnp.where(classes == level, levels_ref[level], density)
    density_ref[...] = density
    modulus_ref[...] = floor_modulus + (1.0 - floor_modulus) * density * density * density

    def piece(p, carry):
        for c in range(3):
            for q in range(9):
                pieces_ref[pl.ds(p * 216 + c * 9 + q, 8, stride=27), :] = x_ref[
                    pl.ds(c * 72 + p * 9 + q, 8, stride=216), :
                ]
        return carry

    lax.fori_loop(0, 8, piece, 0)


def layer(top, bottom):
    s = {k: top[k] + bottom[k] for k in top if k[1] != "00"}
    d = {k: top[k] - bottom[k] for k in top}
    even, odd = {}, {}
    trace = LAME * (s[0, "10"] + s[1, "01"] + d[2, "00"])
    even[0, "10"] = trace + NORMAL * s[0, "10"]
    even[1, "01"] = trace + NORMAL * s[1, "01"]
    odd[2, "00"] = trace + NORMAL * d[2, "00"]
    even[1, "10"] = even[0, "01"] = SHEAR * (s[1, "10"] + s[0, "01"])
    even[2, "10"] = odd[0, "00"] = SHEAR * (s[2, "10"] + d[0, "00"])
    even[2, "01"] = odd[1, "00"] = SHEAR * (s[2, "01"] + d[1, "00"])
    even[0, "11"] = BEND * s[0, "11"] + CROSS * d[2, "01"]
    even[1, "11"] = BEND * s[1, "11"] + CROSS * d[2, "10"]
    twist = TWIST * (s[2, "11"] + d[1, "10"] + d[0, "01"])
    even[2, "11"] = twist + TWIST * s[2, "11"]
    odd[1, "10"] = twist + TWIST * d[1, "10"]
    odd[0, "01"] = twist + TWIST * d[0, "01"]
    odd[0, "10"] = BEND * d[0, "10"] + CROSS * d[1, "01"]
    odd[1, "01"] = BEND * d[1, "01"] + CROSS * d[0, "10"]
    odd[2, "10"] = BEND * d[2, "10"] + CROSS * s[1, "11"]
    odd[2, "01"] = BEND * d[2, "01"] + CROSS * s[0, "11"]
    for c in range(3):
        odd[c, "11"] = LAST * d[c, "11"]
    return even, odd


def element_row(previous, rows, low, high):
    current, planes = [], []
    for p in range(3):
        fields = {}
        for c in range(3):
            u = rows[p][c]
            back = pltpu.roll(u, 1, 1)
            total, diff = u + back, u - back
            old_total, old_diff = previous[p * 3 + c]
            fields[c, "00"] = total + old_total
            fields[c, "10"] = diff + old_diff
            fields[c, "01"] = total - old_total
            fields[c, "11"] = diff - old_diff
            current.append((total, diff))
        planes.append(fields)
    own, below, above = planes
    even, odd = layer(own, below)
    even_up, odd_up = layer(above, own)
    plus, minus = [], []
    for c in range(3):
        f = {}
        for k in ("00", "10", "01", "11"):
            if k == "00":
                f[k] = low * odd[c, k] - high * odd_up[c, k]
            else:
                f[k] = low * (even[c, k] + odd[c, k]) + high * (even_up[c, k] - odd_up[c, k])
        plus.append((f["00"] + f["01"], f["10"] + f["11"]))
        minus.append((f["00"] - f["01"], f["10"] - f["11"]))
    return current, plus, minus


def stiffness_kernel(own, below, above, modulus, modulus_up, out, low_rows, high_rows):
    wide = lane_index(24)
    for source, target in ((modulus, low_rows), (modulus_up, high_rows)):
        chunks = [source[pl.ds(k, 24, stride=3), :] for k in range(3)]
        for k, row in enumerate(rows_of_chunks(*chunks, wide)):
            target[pl.ds(k, 24, stride=4), :] = row
        target[pl.ds(NY, 8), :] = jnp.zeros((8, LANES), jnp.float32)
    lane = lane_index(8)
    planes = (own, below, above)

    def chunk(plane, c, index):
        return plane[pl.ds(c * 72 + index, 8, stride=216), :]

    def moduli(j):
        return tuple(
            jnp.broadcast_to(ref[pl.ds(j, 1), :], (8, LANES)) for ref in (low_rows, high_rows)
        )

    zero = jnp.zeros((8, LANES), jnp.float32)
    first = [[jnp.where(lane < NX, chunk(plane, c, 0), 0.0) for c in range(3)] for plane in planes]
    state, plus, unused = element_row([(zero, zero)] * 9, first, *moduli(0))

    def group(g, carry):
        state, plus = carry
        rows = [[None] * 3 for unused in range(3)]
        for p in range(3):
            for c in range(3):
                v0, v1, v2 = [chunk(planes[p], c, 3 * g + k) for k in range(3)]
                v3 = chunk(planes[p], c, jnp.minimum(3 * g + 3, 71))
                rows[p][c] = rows_of_chunks(v0, v1, v2, lane)[1:] + [jnp.where(lane < NX, v3, 0.0)]
        results = [[] for unused in range(3)]
        for step in range(4):
            here = [[rows[p][c][step] for c in range(3)] for p in range(3)]
            state, new_plus, minus = element_row(state, here, *moduli(4 * g + 1 + step))
            for c in range(3):
                even, odd = plus[c][0] + minus[c][0], plus[c][1] + minus[c][1]
                results[c].append((even + odd) + pltpu.roll(even - odd, LANES - 1, 1))
            plus = new_plus
        base = (g // 3) * 216 + (g % 3) * 3
        for c in range(3):
            for k, v in enumerate(chunks_of_rows(*results[c], lane)):
                out[pl.ds(base + c * 9 + k, 8, stride=27), :] = v
        return state, plus

    lax.fori_loop(0, 24, group, (state, plus))


def gram_kernel(basis, image, density, out):
    acc = jnp.zeros((64, LANES), jnp.float32)
    for c in range(3):
        for q in range(9):
            t = c * 9 + q
            b = basis[pl.ds(t, 64, stride=27), :]
            v = image[pl.ds(t, 64, stride=27), :]
            m = b * density[pl.ds(q, 1), :]
            both = jnp.concatenate([v, m], 0)
            acc = acc + lax.dot_general(
                b, both, (((1,), (1,)), ((), ())), precision=highest, preferred_element_type=jnp.float32
            )
    out[...] = acc


def dot(a, b, dims):
    return lax.dot_general(
        a, b, (dims, ((), ())), precision=highest, preferred_element_type=jnp.float32
    )


def inverse_factor(mass):
    row = lax.broadcasted_iota(jnp.int32, (64, LANES), 0)
    lane = lax.broadcasted_iota(jnp.int32, (64, LANES), 1)
    w = jnp.where(lane < 64, mass, jnp.where(lane - 64 == row, 1.0, 0.0))
    for k in range(0, 64, 2):
        r0, r1 = w[k : k + 1, :], w[k + 1 : k + 2, :]
        c0, c1 = w[:, k : k + 1], w[:, k + 1 : k + 2]
        a, b, d = r0[:, k : k + 1], r0[:, k + 1 : k + 2], r1[:, k + 1 : k + 2]
        inv = 1.0 / (a * d - b * b)
        x0 = (d * r0 - b * r1) * inv
        x1 = (a * r1 - b * r0) * inv
        w = jnp.where(row > k + 1, w - c0 * x0 - c1 * x1, w)
    diagonal = jnp.sum(jnp.where(lane == row, w, 0.0), 1, keepdims=True)
    left = jnp.sum(jnp.where(lane == row - 1, w, 0.0), 1, keepdims=True)
    odd = row % 2 == 1
    up = pltpu.roll(w, 1, 0)
    up_diagonal = pltpu.roll(jnp.broadcast_to(diagonal, (64, LANES)), 1, 0)
    ratio = jnp.where(odd, left / jnp.where(odd, up_diagonal, 1.0), 0.0)
    pivot = diagonal - ratio * left
    scaled = (w - ratio * up) * lax.rsqrt(pivot)
    return scaled[:, 64:]


def residual_kernel(total_dofs, gram, basis, image, density, out, ritz_ref):
    scale = 1.0 / total_dofs
    both = gram[...] * scale
    mass = pltpu.roll(both, 64, 1)
    inverse = inverse_factor(mass)
    stiff = both[:, :64]
    ritz = dot(dot(inverse, stiff, ((1,), (0,))), inverse, ((1,), (1,)))
    ritz_ref[...] = ritz
    mixed = dot(ritz, inverse, ((0,), (0,)))
    weights = jnp.concatenate([inverse, -mixed], 1)
    for c in range(3):
        for q in range(9):
            t = c * 9 + q
            b = basis[pl.ds(t, 64, stride=27), :]
            v = image[pl.ds(t, 64, stride=27), :]
            m = b * density[pl.ds(q, 1), :]
            out[pl.ds(t, 64, stride=27), :] = dot(
                weights, jnp.concatenate([v, m], 0), ((1,), (0,))
            )


def join_kernel(x_ref, out_ref):
    def piece(p, carry):
        for c in range(3):
            for q in range(9):
                out_ref[pl.ds(c * 72 + p * 9 + q, 8, stride=216), :] = x_ref[
                    pl.ds(p * 216 + c * 9 + q, 8, stride=27), :
                ]
        return carry

    lax.fori_loop(0, 8, piece, 0)


def room(mib):
    return pltpu.CompilerParams(vmem_limit_bytes=mib << 20)


def f32(*shape):
    return jax.ShapeDtypeStruct(shape, jnp.float32)


def exchanged(x, axis, mask):
    size = lax.axis_size(axis)
    return lax.ppermute(x, axis, [(i, i ^ mask) for i in range(size)])


def total_sum(x):
    for axis in ("modes_1", ("mesh_0", "modes_0")):
        x = (x + exchanged(x, axis, 1)) + (exchanged(x, axis, 2) + exchanged(x, axis, 3))
    x = x + exchanged(x, "mesh_2", 1)
    for mask in (1, 2, 4):
        x = x + exchanged(x, "mesh_1", mask)
    return x


def per_device(subspace, classes, level_density):
    total_dofs = 3 * NX * NY * subspace.shape[2] * lax.axis_size(MESH)
    flat = subspace.reshape(1728, LANES)
    below = shifted(flat, MESH, 1)
    above = shifted(flat, MESH, -1)
    pieces, density, modulus = pl.pallas_call(
        prep_kernel,
        in_specs=[VMEM, VMEM, SMEM],
        out_specs=[VMEM, VMEM, VMEM],
        out_shape=[f32(1728, LANES), f32(72, LANES), f32(72, LANES)],
        cost_estimate=pl.CostEstimate(flops=10**5, bytes_accessed=1_800_000, transcendentals=0),
        compiler_params=room(8),
        name="prep",
    )(flat, classes.reshape(72, LANES), level_density)
    modulus_up = shifted(modulus, MESH, -1)

    def all_to_all(x):
        x = x.reshape(8, 216, LANES)
        return lax.all_to_all(x, MODES, split_axis=0, concat_axis=0, tiled=True).reshape(1728, LANES)

    basis = all_to_all(pieces)
    image_pieces = pl.pallas_call(
        stiffness_kernel,
        in_specs=[VMEM] * 5,
        out_specs=VMEM,
        out_shape=f32(1728, LANES),
        scratch_shapes=[pltpu.VMEM((104, LANES), jnp.float32)] * 2,
        cost_estimate=pl.CostEstimate(
            flops=27_000_000, bytes_accessed=3_600_000, transcendentals=0
        ),
        compiler_params=room(12),
        name="stiffness",
    )(flat, below, above, modulus, modulus_up)
    image = all_to_all(image_pieces)
    band = lax.axis_index(MODES)
    band_density = lax.dynamic_slice_in_dim(density, band * 9, 9, 0)
    local = pl.pallas_call(
        gram_kernel,
        in_specs=[VMEM] * 3,
        out_specs=VMEM,
        out_shape=f32(64, LANES),
        compiler_params=room(8),
        name="grams",
    )(basis, image, band_density)
    gram = total_sum(local)
    residual_pieces, ritz_matrix = pl.pallas_call(
        functools.partial(residual_kernel, total_dofs),
        in_specs=[VMEM] * 4,
        out_specs=[VMEM, VMEM],
        out_shape=[f32(1728, LANES), f32(64, 64)],
        compiler_params=room(12),
        name="residual",
    )(gram, basis, image, band_density)
    joined = pl.pallas_call(
        join_kernel,
        in_specs=[VMEM],
        out_specs=VMEM,
        out_shape=f32(1728, LANES),
        compiler_params=room(8),
        name="join",
    )(all_to_all(residual_pieces))
    return (joined.reshape(subspace.shape), ritz_matrix)


def solution(mesh):
    split = Mesh(
        mesh.devices.reshape(2, 8, 2, 2, 4), ("mesh_0", "mesh_1", "mesh_2", "modes_0", "modes_1")
    )
    placed = (P(MODES, None, MESH, None), P(MESH, None), P())
    return jax.shard_map(
        per_device,
        mesh=split,
        in_specs=placed,
        out_specs=(P(MODES, None, MESH, None), P()),
        check_vma=False,
    )
```

profile of v0, /device:TPU:32, one launch (start us, length us, event | category | flops | bytes accessed | tf_op | source)
XLA Modules:
  0.0 121.9 jit_solution(12187940569819347677)
XLA Ops:
  0.6 1.9 %collective-permute-start.1 = (f32[1728,128]{1,0:T(8,128)}, f32[1728,128]{1,0:T(8,128)S(1)}, u32[]{:S(2)}, u32[]{:S(2)}) collective-permute-start(f32[1728,128]{1,0:T(8,128)} %bitcast.13), channel_id=1, source_target_pairs={{8,0},{16,8},{24,16},{32,24},{40,32},{48,40},{56,48},{64,56},{72,6... | collective-permute-start | bytes 2654216 | tf_op jit(solution)/shard_map/ppermute | solution.py:27
  2.6 2.4 %collective-permute-start = (f32[1728,128]{1,0:T(8,128)}, f32[1728,128]{1,0:T(8,128)S(1)}, u32[]{:S(2)}, u32[]{:S(2)}) collective-permute-start(f32[1728,128]{1,0:T(8,128)} %bitcast.14), channel_id=1, source_target_pairs={{0,8},{8,16},{16,24},{24,32},{32,40},{40,48},{48,56},{56,64},{64,7... | collective-permute-start | bytes 2654216 | tf_op jit(solution)/shard_map/ppermute | solution.py:27
  5.0 1.2 copy-done
  9.9 7.1 %all-to-all-start = ((f32[8,216,128]{2,1,0:T(8,128)}), f32[8,216,128]{2,1,0:T(8,128)S(1)}, u32[]{:S(2)}, u32[]{:S(2)}) async-start(f32[8,216,128]{2,1,0:T(8,128)} %bitcast.18), calls=%async_computation | async-start | bytes 1769472 | tf_op jit(solution)/shard_map/all_to_all | solution.py:351
  16.9 2.9 %collective-permute-start.2 = (f32[72,128]{1,0:T(8,128)}, f32[72,128]{1,0:T(8,128)S(1)}, u32[]{:S(2)}, u32[]{:S(2)}) collective-permute-start(f32[72,128]{1,0:T(8,128)} %copy-done.3), channel_id=1, source_target_pairs={{8,0},{16,8},{24,16},{32,24},{40,32},{48,40},{56,48},{64,56},{72,6... | collective-permute-start | bytes 110600 | tf_op jit(solution)/shard_map/ppermute | solution.py:27
  19.8 1.9 %collective-permute-done.2.modulus_up = f32[72,128]{1,0:T(8,128)S(1)} collective-permute-done((f32[72,128]{1,0:T(8,128)}, f32[72,128]{1,0:T(8,128)S(1)}, u32[]{:S(2)}, u32[]{:S(2)}) %collective-permute-start.2) | collective-permute-done | bytes 36896 | tf_op jit(solution)/shard_map/ppermute | solution.py:27
  22.5 12.5 %stiffness.1 = f32[1728,128]{1,0:T(8,128)} custom-call(f32[1728,128]{1,0:T(8,128)S(1)} %bitcast.16, f32[1728,128]{1,0:T(8,128)S(1)} %collective-permute-done.below, f32[1728,128]{1,0:T(8,128)S(1)} %collective-permute-done.1.above, f32[72,128]{1,0:T(8,128)S(1)} %copy-done.4, f32[72,128]{1,0:T(8,128)S(1)} %collective-permute-done.2.modulus_up), custom_call_target="tpu_custom_call" | custom-call | flops 27000000 | bytes 3600000 | tf_op jit(solution)/shard_map/stiffness/pallas_call | solution.py:354
  35.0 6.9 %all-to-all-start.1 = ((f32[8,216,128]{2,1,0:T(8,128)}), f32[8,216,128]{2,1,0:T(8,128)S(1)}, u32[]{:S(2)}, u32[]{:S(2)}) async-start(f32[8,216,128]{2,1,0:T(8,128)} %bitcast.4), calls=%async_computation.1 | async-start | bytes 1769472 | tf_op jit(solution)/shard_map/all_to_all | solution.py:351
  42.6 13.1 %all-to-all-done.1 = f32[8,216,128]{2,1,0:T(8,128)S(1)} async-done(((f32[8,216,128]{2,1,0:T(8,128)}), f32[8,216,128]{2,1,0:T(8,128)S(1)}, u32[]{:S(2)}, u32[]{:S(2)}) %all-to-all-start.1) | async-done | bytes 884768 | tf_op jit(solution)/shard_map/all_to_all | solution.py:351
  55.7 3.5 %grams.1 = f32[64,128]{1,0:T(8,128)S(1)} custom-call(f32[1728,128]{1,0:T(8,128)S(1)} %bitcast.9, f32[1728,128]{1,0:T(8,128)S(1)} %bitcast.11, f32[9,128]{1,0:T(8,128)S(1)} %constant_dynamic-slice_fusion.density), custom_call_target="tpu_custom_call" | custom-call | tf_op jit(solution)/shard_map/grams/pallas_call | solution.py:369
  59.2 2.8 %collective-permute-start.5 = (f32[64,128]{1,0:T(8,128)S(1)}, f32[64,128]{1,0:T(8,128)S(1)}, u32[]{:S(2)}, u32[]{:S(2)}) collective-permute-start(f32[64,128]{1,0:T(8,128)S(1)} %grams.1), channel_id=1, source_target_pairs={{0,3},{1,2},{2,1},{3,0},{4,7},{5,6},{6,5},{7,4},{8,11},{9,10},{10,... | collective-permute-start | bytes 98312 | tf_op jit(solution)/shard_map/ppermute | solution.py:321
  64.4 3.2 %collective-permute-done.4 = f32[64,128]{1,0:T(8,128)S(1)} collective-permute-done((f32[64,128]{1,0:T(8,128)S(1)}, f32[64,128]{1,0:T(8,128)S(1)}, u32[]{:S(2)}, u32[]{:S(2)}) %collective-permute-start.4) | collective-permute-done | bytes 32800 | tf_op jit(solution)/shard_map/ppermute | solution.py:321
  67.7 1.9 %collective-permute-start.8 = (f32[64,128]{1,0:T(8,128)S(1)}, f32[64,128]{1,0:T(8,128)S(1)}, u32[]{:S(2)}, u32[]{:S(2)}) collective-permute-start(f32[64,128]{1,0:T(8,128)S(1)} %add_add_fusion.1), channel_id=1, source_target_pairs={{0,132},{4,128},{128,4},{132,0},{1,133},{5,129},{129,5},{133,1},{2... | collective-permute-start | bytes 98312 | tf_op jit(solution)/shard_map/ppermute | solution.py:321
  69.7 2.7 %collective-permute-start.6 = (f32[64,128]{1,0:T(8,128)S(1)}, f32[64,128]{1,0:T(8,128)S(1)}, u32[]{:S(2)}, u32[]{:S(2)}) collective-permute-start(f32[64,128]{1,0:T(8,128)S(1)} %add_add_fusion.1), channel_id=1, source_target_pairs={{0,4},{4,0},{128,132},{132,128},{1,5},{5,1},{129,133},{133,129},{2... | collective-permute-start | bytes 98312 | tf_op jit(solution)/shard_map/ppermute | solution.py:321
  73.4 1.7 %collective-permute-done.6 = f32[64,128]{1,0:T(8,128)S(1)} collective-permute-done((f32[64,128]{1,0:T(8,128)S(1)}, f32[64,128]{1,0:T(8,128)S(1)}, u32[]{:S(2)}, u32[]{:S(2)}) %collective-permute-start.6) | collective-permute-done | bytes 32800 | tf_op jit(solution)/shard_map/ppermute | solution.py:321
  75.3 1.2 collective-permute-done.9
  76.5 2.9 %collective-permute-start.10 = (f32[64,128]{1,0:T(8,128)S(1)}, f32[64,128]{1,0:T(8,128)S(1)}, u32[]{:S(2)}, u32[]{:S(2)}) collective-permute-start(f32[64,128]{1,0:T(8,128)S(1)} %add.44), channel_id=1, source_target_pairs={{0,16},{16,0},{32,48},{48,32},{64,80},{80,64},{96,112},{112,96},{1... | collective-permute-start | bytes 98312 | tf_op jit(solution)/shard_map/ppermute | solution.py:321
  79.4 1.9 %collective-permute-done.10 = f32[64,128]{1,0:T(8,128)S(1)} collective-permute-done((f32[64,128]{1,0:T(8,128)S(1)}, f32[64,128]{1,0:T(8,128)S(1)}, u32[]{:S(2)}, u32[]{:S(2)}) %collective-permute-start.10) | collective-permute-done | bytes 32800 | tf_op jit(solution)/shard_map/ppermute | solution.py:321
  81.3 2.6 %collective-permute-start.11 = (f32[64,128]{1,0:T(8,128)S(1)}, f32[64,128]{1,0:T(8,128)S(1)}, u32[]{:S(2)}, u32[]{:S(2)}) collective-permute-start(f32[64,128]{1,0:T(8,128)S(1)} %add.45), channel_id=1, source_target_pairs={{0,32},{16,48},{32,0},{48,16},{64,96},{80,112},{96,64},{112,80},{1... | collective-permute-start | bytes 98312 | tf_op jit(solution)/shard_map/ppermute | solution.py:321
  83.8 2.3 %collective-permute-done.11 = f32[64,128]{1,0:T(8,128)S(1)} collective-permute-done((f32[64,128]{1,0:T(8,128)S(1)}, f32[64,128]{1,0:T(8,128)S(1)}, u32[]{:S(2)}, u32[]{:S(2)}) %collective-permute-start.11) | collective-permute-done | bytes 32800 | tf_op jit(solution)/shard_map/ppermute | solution.py:321
  86.1 6.1 %collective-permute-start.12 = (f32[64,128]{1,0:T(8,128)S(1)}, f32[64,128]{1,0:T(8,128)S(1)}, u32[]{:S(2)}, u32[]{:S(2)}) collective-permute-start(f32[64,128]{1,0:T(8,128)S(1)} %add.46), channel_id=1, source_target_pairs={{0,64},{16,80},{32,96},{48,112},{64,0},{80,16},{96,32},{112,48},{1... | collective-permute-start | bytes 98312 | tf_op jit(solution)/shard_map/ppermute | solution.py:321
  92.2 1.9 %collective-permute-done.12 = f32[64,128]{1,0:T(8,128)S(1)} collective-permute-done((f32[64,128]{1,0:T(8,128)S(1)}, f32[64,128]{1,0:T(8,128)S(1)}, u32[]{:S(2)}, u32[]{:S(2)}) %collective-permute-start.12) | collective-permute-done | bytes 32800 | tf_op jit(solution)/shard_map/ppermute | solution.py:321
  94.1 7.8 %residual.1 = (f32[1728,128]{1,0:T(8,128)S(1)}, f32[64,64]{1,0:T(8,128)}) custom-call(f32[64,128]{1,0:T(8,128)S(1)} %add.47.gram, f32[1728,128]{1,0:T(8,128)S(1)} %bitcast.10, f32[1728,128]{1,0:T(8,128)S(1)} %bitcast.12, f32[9,128]{1,0:T(8,128)S(1)} %constant_dynamic-slice_fusion.density), custom_call_target="tpu_custom_call" | custom-call | tf_op jit(solution)/shard_map/residual/pallas_call | solution.py:378
  101.8 19.0 %all_to_all.15 = f32[8,216,128]{2,1,0:T(8,128)S(1)} all-to-all(f32[8,216,128]{2,1,0:T(8,128)S(1)} %bitcast.19), channel_id=1, replica_groups=mesh['mesh_0'=2,'mesh_1'=8,'mesh_2'=2,'modes_0'=2,'modes_1'=4] {'modes_0..., dimensions={0} | all-to-all | bytes 1769472 | tf_op jit(solution)/shard_map/all_to_all | solution.py:351
  (35 shorter events, 10.0 us)
Async XLA Ops:
  0.6 4.4 %copy-start.7 = (f32[16]{0:T(128)S(1)}, f32[16]{0:T(128)}, u32[]{:S(2)}) copy-start(f32[16]{0:T(128)} %levels_ref.1) | copy-start | bytes 196
  0.6 21.1 %collective-permute-start.1 = (f32[1728,128]{1,0:T(8,128)}, f32[1728,128]{1,0:T(8,128)S(1)}, u32[]{:S(2)}, u32[]{:S(2)}) collective-permute-start(f32[1728,128]{1,0:T(8,128)} %bitcast.13), channel_id=1, source_target_pairs={{8,0},{16,8},{24,16},{32,24},{40,32},{48,40},{56,48},{64,56},{72,6... | collective-permute-start | bytes 2654216 | tf_op jit(solution)/shard_map/ppermute | solution.py:27
  2.6 19.2 %collective-permute-start = (f32[1728,128]{1,0:T(8,128)}, f32[1728,128]{1,0:T(8,128)S(1)}, u32[]{:S(2)}, u32[]{:S(2)}) collective-permute-start(f32[1728,128]{1,0:T(8,128)} %bitcast.14), channel_id=1, source_target_pairs={{0,8},{8,16},{16,24},{24,32},{32,40},{40,48},{48,56},{56,64},{64,7... | collective-permute-start | bytes 2654216 | tf_op jit(solution)/shard_map/ppermute | solution.py:27
  5.0 1.2 copy-start
  6.2 0.8 copy-start.5
  7.7 0.9 copy-start.2
  8.6 0.6 copy-start.3
  9.2 0.6 copy-start.6
  9.9 11.9 %copy-start.1 = (f32[8,3,1,9216]{3,2,1,0:T(1,128)S(1)}, f32[8,3,1,9216]{3,2,1,0:T(1,128)}, u32[]{:S(2)}) copy-start(f32[8,3,1,9216]{3,2,1,0:T(1,128)} %param.3) | copy-start | bytes 2654212
  9.9 25.1 %all-to-all-start = ((f32[8,216,128]{2,1,0:T(8,128)}), f32[8,216,128]{2,1,0:T(8,128)S(1)}, u32[]{:S(2)}, u32[]{:S(2)}) async-start(f32[8,216,128]{2,1,0:T(8,128)} %bitcast.18), calls=%async_computation | async-start | bytes 1769472 | tf_op jit(solution)/shard_map/all_to_all | solution.py:351
  16.9 4.8 %collective-permute-start.2 = (f32[72,128]{1,0:T(8,128)}, f32[72,128]{1,0:T(8,128)S(1)}, u32[]{:S(2)}, u32[]{:S(2)}) collective-permute-start(f32[72,128]{1,0:T(8,128)} %copy-done.3), channel_id=1, source_target_pairs={{8,0},{16,8},{24,16},{32,24},{40,32},{48,40},{56,48},{64,56},{72,6... | collective-permute-start | bytes 110600 | tf_op jit(solution)/shard_map/ppermute | solution.py:27
  21.7 0.8 copy-start.4
  35.0 20.8 %all-to-all-start.1 = ((f32[8,216,128]{2,1,0:T(8,128)}), f32[8,216,128]{2,1,0:T(8,128)S(1)}, u32[]{:S(2)}, u32[]{:S(2)}) async-start(f32[8,216,128]{2,1,0:T(8,128)} %bitcast.4), calls=%async_computation.1 | async-start | bytes 1769472 | tf_op jit(solution)/shard_map/all_to_all | solution.py:351
  59.2 5.2 %collective-permute-start.5 = (f32[64,128]{1,0:T(8,128)S(1)}, f32[64,128]{1,0:T(8,128)S(1)}, u32[]{:S(2)}, u32[]{:S(2)}) collective-permute-start(f32[64,128]{1,0:T(8,128)S(1)} %grams.1), channel_id=1, source_target_pairs={{0,3},{1,2},{2,1},{3,0},{4,7},{5,6},{6,5},{7,4},{8,11},{9,10},{10,... | collective-permute-start | bytes 98312 | tf_op jit(solution)/shard_map/ppermute | solution.py:321
  62.0 5.7 %collective-permute-start.4 = (f32[64,128]{1,0:T(8,128)S(1)}, f32[64,128]{1,0:T(8,128)S(1)}, u32[]{:S(2)}, u32[]{:S(2)}) collective-permute-start(f32[64,128]{1,0:T(8,128)S(1)} %grams.1), channel_id=1, source_target_pairs={{0,2},{1,3},{2,0},{3,1},{4,6},{5,7},{6,4},{7,5},{8,10},{9,11},{10,... | collective-permute-start | bytes 98312 | tf_op jit(solution)/shard_map/ppermute | solution.py:321
  62.8 4.8 %collective-permute-start.3 = (f32[64,128]{1,0:T(8,128)S(1)}, f32[64,128]{1,0:T(8,128)S(1)}, u32[]{:S(2)}, u32[]{:S(2)}) collective-permute-start(f32[64,128]{1,0:T(8,128)S(1)} %grams.1), channel_id=1, source_target_pairs={{0,1},{1,0},{2,3},{3,2},{4,5},{5,4},{6,7},{7,6},{8,9},{9,8},{10,11... | collective-permute-start | bytes 98312 | tf_op jit(solution)/shard_map/ppermute | solution.py:321
  67.7 5.2 %collective-permute-start.8 = (f32[64,128]{1,0:T(8,128)S(1)}, f32[64,128]{1,0:T(8,128)S(1)}, u32[]{:S(2)}, u32[]{:S(2)}) collective-permute-start(f32[64,128]{1,0:T(8,128)S(1)} %add_add_fusion.1), channel_id=1, source_target_pairs={{0,132},{4,128},{128,4},{132,0},{1,133},{5,129},{129,5},{133,1},{2... | collective-permute-start | bytes 98312 | tf_op jit(solution)/shard_map/ppermute | solution.py:321
  69.5 3.9 %collective-permute-start.7 = (f32[64,128]{1,0:T(8,128)S(1)}, f32[64,128]{1,0:T(8,128)S(1)}, u32[]{:S(2)}, u32[]{:S(2)}) collective-permute-start(f32[64,128]{1,0:T(8,128)S(1)} %add_add_fusion.1), channel_id=1, source_target_pairs={{0,128},{4,132},{128,0},{132,4},{1,129},{5,133},{129,1},{133,5},{2... | collective-permute-start | bytes 98312 | tf_op jit(solution)/shard_map/ppermute | solution.py:321
  69.7 5.4 %collective-permute-start.6 = (f32[64,128]{1,0:T(8,128)S(1)}, f32[64,128]{1,0:T(8,128)S(1)}, u32[]{:S(2)}, u32[]{:S(2)}) collective-permute-start(f32[64,128]{1,0:T(8,128)S(1)} %add_add_fusion.1), channel_id=1, source_target_pairs={{0,4},{4,0},{128,132},{132,128},{1,5},{5,1},{129,133},{133,129},{2... | collective-permute-start | bytes 98312 | tf_op jit(solution)/shard_map/ppermute | solution.py:321
  75.2 1.3 %collective-permute-start.9 = (f32[64,128]{1,0:T(8,128)S(1)}, f32[64,128]{1,0:T(8,128)S(1)}, u32[]{:S(2)}, u32[]{:S(2)}) collective-permute-start(f32[64,128]{1,0:T(8,128)S(1)} %add_add_fusion), channel_id=1, source_target_pairs={{0,8},{8,0},{1,9},{9,1},{2,10},{10,2},{3,11},{11,3},{4,12},{12,4},... | collective-permute-start | bytes 98312 | tf_op jit(solution)/shard_map/ppermute | solution.py:321
  76.5 4.8 %collective-permute-start.10 = (f32[64,128]{1,0:T(8,128)S(1)}, f32[64,128]{1,0:T(8,128)S(1)}, u32[]{:S(2)}, u32[]{:S(2)}) collective-permute-start(f32[64,128]{1,0:T(8,128)S(1)} %add.44), channel_id=1, source_target_pairs={{0,16},{16,0},{32,48},{48,32},{64,80},{80,64},{96,112},{112,96},{1... | collective-permute-start | bytes 98312 | tf_op jit(solution)/shard_map/ppermute | solution.py:321
  81.3 4.8 %collective-permute-start.11 = (f32[64,128]{1,0:T(8,128)S(1)}, f32[64,128]{1,0:T(8,128)S(1)}, u32[]{:S(2)}, u32[]{:S(2)}) collective-permute-start(f32[64,128]{1,0:T(8,128)S(1)} %add.45), channel_id=1, source_target_pairs={{0,32},{16,48},{32,0},{48,16},{64,96},{80,112},{96,64},{112,80},{1... | collective-permute-start | bytes 98312 | tf_op jit(solution)/shard_map/ppermute | solution.py:321
  86.1 8.0 %collective-permute-start.12 = (f32[64,128]{1,0:T(8,128)S(1)}, f32[64,128]{1,0:T(8,128)S(1)}, u32[]{:S(2)}, u32[]{:S(2)}) collective-permute-start(f32[64,128]{1,0:T(8,128)S(1)} %add.46), channel_id=1, source_target_pairs={{0,64},{16,80},{32,96},{48,112},{64,0},{80,16},{96,32},{112,48},{1... | collective-permute-start | bytes 98312 | tf_op jit(solution)/shard_map/ppermute | solution.py:321
where the time goes:
time: 122 us
  starting transfers between devices  41.8 us (34%)
  waiting for transfers between devices  29.3 us (24%)
  Pallas kernels  25.6 us (21%)
  blocking collectives  19 us (16%)
  local copies, waits for them, and re-layouts  5.53 us (5%)
    ppermute x10, starting transfers between devices, exchanged(): return lax.ppermute(x, axis, [(i, i ^ mask) for i in range(size)])  20.6 us
    all_to_all x1, blocking collectives, all_to_all(): lax.all_to_all(x, MODES, split_axis=0, concat_axis=0, tiled=True)  19 us
    ppermute x10, waiting for transfers between devices, exchanged(): return lax.ppermute(x, axis, [(i, i ^ mask) for i in range(size)])  14.2 us
    all_to_all x2, starting transfers between devices, all_to_all(): lax.all_to_all(x, MODES, split_axis=0, concat_axis=0, tiled=True)  14 us
    all_to_all x2, waiting for transfers between devices, all_to_all(): lax.all_to_all(x, MODES, split_axis=0, concat_axis=0, tiled=True)  13.1 us
    pallas_call x1, Pallas kernels, per_device(): pl.pallas_call(stiffness_kernel, in_specs=[VMEM] * 5, out_specs=VMEM, out...  12.5 us
    pallas_call x1, Pallas kernels, per_device(): pl.pallas_call(functools.partial(residual_kernel, total_dofs), in_specs=[...  7.76 us
    ppermute x3, starting transfers between devices, shifted(): return lax.ppermute(x, axis, pairs)  7.19 us
  transfers between devices with their start and end apart: 15, of which 11 were waited for; matrix products, arithmetic and copies ran while one was open for 1% of the time, Pallas kernels for 11%

commit v1 on v0

v1 whole, which is shorter than its diff:
```python
import functools

import jax
import jax.numpy as jnp
import numpy as np
from jax import lax
from jax.experimental import pallas as pl
from jax.experimental.pallas import tpu as pltpu
from jax.sharding import Mesh
from jax.sharding import PartitionSpec as P


NX = 96
NY = 96
LANES = 128
MODES = ("modes_0", "modes_1")
MESH = ("mesh_0", "mesh_1", "mesh_2")

highest = lax.Precision.HIGHEST
floor_modulus = 0.001
VMEM = pl.BlockSpec(memory_space=pltpu.VMEM)
SMEM = pl.BlockSpec(memory_space=pltpu.SMEM)
HBM = pl.BlockSpec(memory_space=pltpu.HBM)


def shifted(x, axis, by):
    size = lax.axis_size(axis)
    pairs = [(i, i + by) for i in range(size) if 0 <= i + by < size]
    return lax.ppermute(x, axis, pairs)


def element_matrix():
    poisson_ratio = 0.3
    lame_first = poisson_ratio / ((1 + poisson_ratio) * (1 - 2 * poisson_ratio))
    shear_modulus = 1.0 / (2 * (1 + poisson_ratio))
    elastic = np.zeros((6, 6))
    elastic[:3, :3] = lame_first
    for normal_index in range(3):
        elastic[normal_index, normal_index] = lame_first + 2 * shear_modulus
        elastic[normal_index + 3, normal_index + 3] = shear_modulus
    corner_signs = [
        (1 - 2 * (corner & 1), 1 - 2 * (corner >> 1 & 1), 1 - 2 * (corner >> 2))
        for corner in range(8)
    ]
    gauss_point = 1.0 / np.sqrt(3.0)
    matrix = np.zeros((24, 24))
    for gauss_x in (-gauss_point, gauss_point):
        for gauss_y in (-gauss_point, gauss_point):
            for gauss_z in (-gauss_point, gauss_point):
                strain = np.zeros((6, 24))
                for corner in range(8):
                    sign_x, sign_y, sign_z = corner_signs[corner]
                    deriv_x = 2 * sign_x * (1 + sign_y * gauss_y) * (1 + sign_z * gauss_z) / 8
                    deriv_y = 2 * sign_y * (1 + sign_x * gauss_x) * (1 + sign_z * gauss_z) / 8
                    deriv_z = 2 * sign_z * (1 + sign_x * gauss_x) * (1 + sign_y * gauss_y) / 8
                    column = 3 * corner
                    strain[0, column] = deriv_x
                    strain[1, column + 1] = deriv_y
                    strain[2, column + 2] = deriv_z
                    strain[3, column] = deriv_y
                    strain[3, column + 1] = deriv_x
                    strain[4, column + 1] = deriv_z
                    strain[4, column + 2] = deriv_y
                    strain[5, column] = deriv_z
                    strain[5, column + 2] = deriv_x
                matrix = matrix + strain.T @ elastic @ strain / 8
    return matrix.reshape(8, 3, 8, 3)


def parity_coefficients():
    signs = np.array([[(-1.0) ** bin(p & n).count("1") for n in range(8)] for p in range(8)])
    block = np.einsum("qn,ncmd,pm->qcpd", signs, element_matrix(), signs) / 64
    unit = block[3, 0, 6, 2]
    ratios = tuple(
        float(np.float32(v / unit))
        for v in (
            block[1, 0, 2, 1],
            block[1, 0, 1, 0] - block[1, 0, 2, 1],
            block[1, 1, 1, 1],
            block[3, 0, 3, 0],
            block[3, 2, 5, 1],
            block[7, 0, 7, 0],
        )
    )
    return (float(np.float32(unit)), *ratios)


UNIT, LAME, NORMAL, SHEAR, BEND, TWIST, LAST = parity_coefficients()


def lane_index(rows):
    return lax.broadcasted_iota(jnp.int32, (rows, LANES), 1)


def modulus_of(density):
    return floor_modulus + (1.0 - floor_modulus) * density * density * density


def densities(classes, levels):
    density = jnp.zeros(classes.shape, jnp.float32)
    for level in range(16):
        density = jnp.where(classes == level, levels[level], density)
    return density


def split_kernel(x_hbm, pieces_hbm, x_ref, pieces_ref, load, store):
    loads = [
        pltpu.make_async_copy(x_hbm.at[:, c], x_ref.at[c], load.at[c]) for c in range(3)
    ]
    for copy in loads:
        copy.start()
    stores = []
    for c in range(3):
        loads[c].wait()
        for p in range(8):
            for q in range(9):
                pieces_ref[pl.ds(p * 216 + c * 9 + q, 8, stride=27), :] = x_ref[
                    c, :, p * 9 + q, :
                ]
            if c == 2:
                part = pl.ds(p * 216, 216)
                stores.append(
                    pltpu.make_async_copy(pieces_ref.at[part], pieces_hbm.at[part], store.at[p])
                )
                stores[-1].start()
    for copy in stores:
        copy.wait()


def layer(top, bottom):
    s = {k: top[k] + bottom[k] for k in top if k[1] != "00"}
    d = {k: top[k] - bottom[k] for k in top}
    even, odd = {}, {}
    trace = LAME * (s[0, "10"] + s[1, "01"] + d[2, "00"])
    even[0, "10"] = trace + NORMAL * s[0, "10"]
    even[1, "01"] = trace + NORMAL * s[1, "01"]
    odd[2, "00"] = trace + NORMAL * d[2, "00"]
    even[1, "10"] = even[0, "01"] = SHEAR * (s[1, "10"] + s[0, "01"])
    even[2, "10"] = odd[0, "00"] = SHEAR * (s[2, "10"] + d[0, "00"])
    even[2, "01"] = odd[1, "00"] = SHEAR * (s[2, "01"] + d[1, "00"])
    even[0, "11"] = BEND * s[0, "11"] + d[2, "01"]
    even[1, "11"] = BEND * s[1, "11"] + d[2, "10"]
    twist = s[2, "11"] + d[1, "10"] + d[0, "01"]
    even[2, "11"] = TWIST * (twist + s[2, "11"])
    odd[1, "10"] = TWIST * (twist + d[1, "10"])
    odd[0, "01"] = TWIST * (twist + d[0, "01"])
    odd[0, "10"] = BEND * d[0, "10"] + d[1, "01"]
    odd[1, "01"] = BEND * d[1, "01"] + d[0, "10"]
    odd[2, "10"] = BEND * d[2, "10"] + s[1, "11"]
    odd[2, "01"] = BEND * d[2, "01"] + s[0, "11"]
    for c in range(3):
        odd[c, "11"] = LAST * d[c, "11"]
    return even, odd


PARITIES = ("00", "10", "01", "11")


def stiffness_kernel(
    own, below, above, classes, classes_up, levels, out, low, high, even_buf, odd_buf, sums, ends
):
    low[...] = UNIT * modulus_of(densities(classes[...], levels))
    is_top = lax.axis_index(MESH) == lax.axis_size(MESH) - 1
    high[...] = modulus_of(densities(classes_up[...], levels)) * jnp.where(is_top, 0.0, UNIT)
    lane = lane_index(8)
    inside = ((lane != 0) & (lane != 96), lane != 64, lane != 32)
    before_end = (lane != 95, lane != 63, (lane != 31) & (lane != 127))
    planes = (own, below, above)

    def forward(g, buf):
        for p in range(3):
            for c in range(3):
                s = p * 3 + c
                old = sums[2 * s], sums[2 * s + 1]
                runs = [planes[p][pl.ds(c * 72 + 3 * g + k, 8, stride=216), :] for k in range(3)]
                rolled = [pltpu.roll(u, 1, 1) for u in runs]
                for k in range(3):
                    back = jnp.where(inside[k], rolled[k], 0.0)
                    if k:
                        back = jnp.where(lane == 0, rolled[k - 1], back)
                    total, diff = runs[k] + back, runs[k] - back
                    new = pltpu.roll(total, 96, 1), pltpu.roll(diff, 96, 1)
                    row_total = jnp.where(lane < 96, old[0], new[0])
                    row_diff = jnp.where(lane < 96, old[1], new[1])
                    old = new
                    base = k * 36 + s * 4
                    buf[base] = total + row_total
                    buf[base + 1] = diff + row_diff
                    buf[base + 2] = total - row_total
                    buf[base + 3] = diff - row_diff
                sums[2 * s], sums[2 * s + 1] = old

    def store(run, c, value):
        row = lax.div(run, 9) * 216 + lax.rem(run, 9) + c * 9
        out[pl.ds(row, 8, stride=27), :] = value

    def inverse(g, buf):
        kept, moved = [], []
        for k in range(3):
            own_f, below_f, above_f = [
                {
                    (c, name): buf[k * 36 + (p * 3 + c) * 4 + n]
                    for c in range(3)
                    for n, name in enumerate(PARITIES)
                }
                for p in range(3)
            ]
            even, odd = layer(own_f, below_f)
            even_up, odd_up = layer(above_f, own_f)
            weight = jnp.broadcast_to(low[pl.ds(3 * g + k, 1), :], (8, LANES))
            weight_up = jnp.broadcast_to(high[pl.ds(3 * g + k, 1), :], (8, LANES))
            keep, move = [], []
            for c in range(3):
                f = {"00": weight * odd[c, "00"] - weight_up * odd_up[c, "00"]}
                for n in PARITIES[1:]:
                    f[n] = weight * (even[c, n] + odd[c, n]) + weight_up * (
                        even_up[c, n] - odd_up[c, n]
                    )
                keep.append((f["00"] + f["10"], f["01"] + f["11"]))
                move.append(
                    [pltpu.roll(v, 127, 1) for v in (f["00"] - f["10"], f["01"] - f["11"])]
                )
            kept.append(keep)
            moved.append(move)
        for c in range(3):
            old_plus, old_minus = ends[2 * c], ends[2 * c + 1]
            for k in range(3):
                pair = []
                for y in range(2):
                    from_right = jnp.where(before_end[k], moved[k][c][y], 0.0)
                    if k < 2:
                        from_right = jnp.where(lane == 127, moved[k + 1][c][y], from_right)
                    pair.append(kept[k][c][y] + from_right)
                plus, minus = pair[0] + pair[1], pltpu.roll(pair[0] - pair[1], 32, 1)
                store(
                    jnp.maximum(3 * g + k - 1, 0),
                    c,
                    old_plus + jnp.where(lane < 32, old_minus, minus),
                )
                old_plus, old_minus = plus, minus
            ends[2 * c], ends[2 * c + 1] = old_plus, old_minus

    zero = jnp.zeros((8, LANES), jnp.float32)
    for k in range(18):
        sums[k] = zero
    for k in range(6):
        ends[k] = zero
    forward(0, even_buf)

    def two_groups(h, carry):
        forward(2 * h + 1, odd_buf)
        inverse(2 * h, even_buf)
        forward(jnp.minimum(2 * h + 2, 23), even_buf)
        inverse(2 * h + 1, odd_buf)
        return carry

    lax.fori_loop(0, 12, two_groups, 0)
    for c in range(3):
        store(71, c, ends[2 * c] + jnp.where(lane < 32, ends[2 * c + 1], 0.0))


def mass_kernel(basis, classes, levels, mass, band_density, density):
    density[...] = densities(classes[...], levels)
    band = lax.axis_index(MODES)
    acc = jnp.zeros((64, 64), jnp.float32)
    for q in range(9):
        row = density[pl.ds(band * 9 + q, 1), :]
        band_density[pl.ds(q, 1), :] = row
        for c in range(3):
            b = basis[pl.ds(c * 9 + q, 64, stride=27), :]
            acc = acc + dot(b, b * row, ((1,), (1,)))
    mass[...] = acc


def square_index():
    row = lax.broadcasted_iota(jnp.int32, (64, 64), 0)
    return row, lax.broadcasted_iota(jnp.int32, (64, 64), 1)


def gram_kernel(basis, image, mass, out):
    acc = jnp.zeros((64, 64), jnp.float32)
    for t in range(27):
        b = basis[pl.ds(t, 64, stride=27), :]
        v = image[pl.ds(t, 64, stride=27), :]
        acc = acc + dot(b, v, ((1,), (1,)))
    row, column = square_index()
    mass = mass[...]
    packed = jnp.where(row >= column, acc, mass)
    diagonal = jnp.sum(jnp.where(row == column, mass, 0.0), 0, keepdims=True)
    top = jnp.concatenate([packed[:32], packed[32:]], 1)
    last = jnp.broadcast_to(jnp.concatenate([diagonal, diagonal], 1), (8, LANES))
    block = jnp.concatenate([top, last], 0)
    for k in range(16):
        out[k] = block


def unpacked(block):
    row, column = square_index()
    packed = jnp.concatenate([block[:32, :64], block[:32, 64:]], 0)
    other = jnp.transpose(packed)
    diagonal = jnp.broadcast_to(block[32:33, :64], (64, 64))
    stiff = jnp.where(row >= column, packed, other)
    mass = jnp.where(row == column, diagonal, jnp.where(row < column, packed, other))
    return stiff, mass


def dot(a, b, dims):
    return lax.dot_general(
        a, b, (dims, ((), ())), precision=highest, preferred_element_type=jnp.float32
    )


def inverse_factor(mass):
    row = lax.broadcasted_iota(jnp.int32, (64, LANES), 0)
    lane = lax.broadcasted_iota(jnp.int32, (64, LANES), 1)
    w = jnp.where(
        lane < 64,
        jnp.concatenate([mass, mass], 1),
        jnp.where(lane - 64 == row, 1.0, 0.0),
    )
    for k in range(0, 64, 2):
        r0, r1 = w[k : k + 1, :], w[k + 1 : k + 2, :]
        c0, c1 = w[:, k : k + 1], w[:, k + 1 : k + 2]
        a, b, d = r0[:, k : k + 1], r0[:, k + 1 : k + 2], r1[:, k + 1 : k + 2]
        inv = 1.0 / (a * d - b * b)
        x0 = (d * r0 - b * r1) * inv
        x1 = (a * r1 - b * r0) * inv
        w = jnp.where(row > k + 1, w - c0 * x0 - c1 * x1, w)
    diagonal = jnp.sum(jnp.where(lane == row, w, 0.0), 1, keepdims=True)
    left = jnp.sum(jnp.where(lane == row - 1, w, 0.0), 1, keepdims=True)
    odd = row % 2 == 1
    up = pltpu.roll(w, 1, 0)
    up_diagonal = pltpu.roll(jnp.broadcast_to(diagonal, (64, LANES)), 1, 0)
    ratio = jnp.where(odd, left / jnp.where(odd, up_diagonal, 1.0), 0.0)
    pivot = diagonal - ratio * left
    scaled = (w - ratio * up) * lax.rsqrt(pivot)
    return scaled[:, 64:]


def residual_kernel(total_dofs, gram, basis, image, density, out, ritz_ref):
    scale = 1.0 / total_dofs
    stiff, mass = unpacked(gram[...] * scale)
    inverse = inverse_factor(mass)
    ritz = dot(dot(inverse, stiff, ((1,), (0,))), inverse, ((1,), (1,)))
    ritz_ref[...] = ritz
    mixed = dot(ritz, inverse, ((0,), (0,)))
    weights = jnp.concatenate([inverse, -mixed], 1)
    for c in range(3):
        for q in range(9):
            t = c * 9 + q
            b = basis[pl.ds(t, 64, stride=27), :]
            v = image[pl.ds(t, 64, stride=27), :]
            m = b * density[pl.ds(q, 1), :]
            out[pl.ds(t, 64, stride=27), :] = dot(
                weights, jnp.concatenate([v, m], 0), ((1,), (0,))
            )


def join_kernel(x_ref, out_ref):
    def piece(p, carry):
        for c in range(3):
            for q in range(9):
                out_ref[pl.ds(c * 72 + p * 9 + q, 8, stride=216), :] = x_ref[
                    pl.ds(p * 216 + c * 9 + q, 8, stride=27), :
                ]
        return carry

    lax.fori_loop(0, 8, piece, 0)


def room(mib):
    return pltpu.CompilerParams(vmem_limit_bytes=mib << 20)


def f32(*shape):
    return jax.ShapeDtypeStruct(shape, jnp.float32)


def total_sum(x):
    layer_axes = ("mesh_0", "modes_0", "modes_1")
    x = jnp.sum(lax.all_to_all(x, layer_axes, split_axis=0, concat_axis=0, tiled=True), 0)
    x = x + lax.ppermute(x, "mesh_2", [(0, 1), (1, 0)])
    x = jnp.broadcast_to(x[None], (8, *x.shape))
    return jnp.sum(lax.all_to_all(x, "mesh_1", split_axis=0, concat_axis=0, tiled=True), 0)


def per_device(subspace, classes, level_density):
    total_dofs = 3 * NX * NY * subspace.shape[2] * lax.axis_size(MESH)
    flat = subspace.reshape(1728, LANES)
    classes = classes.reshape(72, LANES)
    below = shifted(flat, MESH, 1)
    above = shifted(flat, MESH, -1)
    classes_up = shifted(classes, MESH, -1)
    split = pl.pallas_call(
        split_kernel,
        in_specs=[HBM],
        out_specs=HBM,
        out_shape=f32(1728, LANES),
        scratch_shapes=[
            pltpu.VMEM((3, 8, 72, LANES), jnp.float32),
            pltpu.VMEM((1728, LANES), jnp.float32),
            pltpu.SemaphoreType.DMA((3,)),
            pltpu.SemaphoreType.DMA((8,)),
        ],
        compiler_params=room(4),
        cost_estimate=pl.CostEstimate(flops=10**5, bytes_accessed=1_800_000, transcendentals=0),
        name="split",
    )
    pieces = split(pltpu.with_memory_space_constraint(flat.reshape(8, 3, 72, LANES), pltpu.HBM))

    def all_to_all(x):
        x = x.reshape(8, 216, LANES)
        return lax.all_to_all(x, MODES, split_axis=0, concat_axis=0, tiled=True).reshape(1728, LANES)

    basis = all_to_all(pieces)
    image_pieces = pl.pallas_call(
        stiffness_kernel,
        in_specs=[VMEM] * 5 + [SMEM],
        out_specs=VMEM,
        out_shape=f32(1728, LANES),
        scratch_shapes=[pltpu.VMEM((72, LANES), jnp.float32)] * 2
        + [pltpu.VMEM((n, 8, LANES), jnp.float32) for n in (108, 108, 18, 6)],
        compiler_params=room(12),
        cost_estimate=pl.CostEstimate(
            flops=27_000_000, bytes_accessed=3_600_000, transcendentals=0
        ),
        name="stiffness",
    )(flat, below, above, classes, classes_up, level_density)
    image = all_to_all(image_pieces)
    mass, band_density = pl.pallas_call(
        mass_kernel,
        in_specs=[VMEM, VMEM, SMEM],
        out_specs=[VMEM, VMEM],
        out_shape=[f32(64, 64), f32(16, LANES)],
        scratch_shapes=[pltpu.VMEM((72, LANES), jnp.float32)],
        compiler_params=room(8),
        cost_estimate=pl.CostEstimate(flops=10**8, bytes_accessed=900_000, transcendentals=0),
        name="mass",
    )(basis, classes, level_density)
    local = pl.pallas_call(
        gram_kernel,
        in_specs=[VMEM] * 3,
        out_specs=VMEM,
        out_shape=f32(16, 40, LANES),
        compiler_params=room(8),
        name="grams",
    )(basis, image, mass)
    gram = total_sum(local)
    residual_pieces, ritz_matrix = pl.pallas_call(
        functools.partial(residual_kernel, total_dofs),
        in_specs=[VMEM] * 4,
        out_specs=[VMEM, VMEM],
        out_shape=[f32(1728, LANES), f32(64, 64)],
        compiler_params=room(12),
        name="residual",
    )(gram, basis, image, band_density)
    joined = pl.pallas_call(
        join_kernel,
        in_specs=[VMEM],
        out_specs=VMEM,
        out_shape=f32(1728, LANES),
        compiler_params=room(8),
        name="join",
    )(all_to_all(residual_pieces))
    return (joined.reshape(subspace.shape), ritz_matrix)


def solution(mesh):
    split = Mesh(
        mesh.devices.reshape(2, 8, 2, 2, 4), ("mesh_0", "mesh_1", "mesh_2", "modes_0", "modes_1")
    )
    placed = (P(MODES, None, MESH, None), P(MESH, None), P())
    return jax.shard_map(
        per_device,
        mesh=split,
        in_specs=placed,
        out_specs=(P(MODES, None, MESH, None), P()),
        check_vma=False,
    )
```

time: 122 us -> 115 us (0.943); the launches traced: 122 us -> 113 us
  blocking collectives: 19 us -> 49 us
  starting transfers between devices: 41.8 us -> 22.1 us
  waiting for transfers between devices: 29.3 us -> 14.8 us
  local copies, waits for them, and re-layouts: 5.53 us -> 0.79 us
    all_to_all x0 -> x2, blocking collectives: none -> 32 us  [the longest x1 17 us: total_sum(): lax.all_to_all(x, 'mesh_1', split_axis=0, concat_axis=0, tiled=True)]
    ppermute x10 -> x1, starting transfers between devices: 20.6 us -> 0.09 us  [total_sum(): x = x + lax.ppermute(x, 'mesh_2', [(0, 1), (1, 0)])]
    ppermute x10 -> x1, waiting for transfers between devices: 14.2 us -> 1.18 us  [total_sum(): x = x + lax.ppermute(x, 'mesh_2', [(0, 1), (1, 0)])]
    unnamed x16 -> x8, local copies, waits for them, and re-layouts: 4.82 us -> 0.78 us
    all_to_all x1, blocking collectives: 19 us -> 17 us  [all_to_all(): lax.all_to_all(x, MODES, split_axis=0, concat_axis=0, tiled=True)]
    pallas_call x2 -> x3, Pallas kernels: 13.2 us -> 15.2 us  [the longest x1 10.8 us: per_device(): pl.pallas_call(stiffness_kernel, in_specs=[VMEM] * 5 + [SMEM], out_specs=...]
    pallas_call x1, Pallas kernels: 3.49 us -> 1.58 us  [per_device(): pl.pallas_call(gram_kernel, in_specs=[VMEM] * 3, out_specs=VMEM, out_shap...]
    all_to_all x2, waiting for transfers between devices: 13.1 us -> 11.7 us  [all_to_all(): lax.all_to_all(x, MODES, split_axis=0, concat_axis=0, tiled=True)]
  transfers between devices with their start and end apart: 15 -> 6, of which waited for: 11 -> 3; matrix products, arithmetic and copies ran while one was open for 1% -> 0% of each run, Pallas kernels for 11% -> 13%
where the time goes in v1:
time: 115 us; the launch traced here: 113 us
  blocking collectives  49 us (43%)
  Pallas kernels  25.8 us (22%)
  starting transfers between devices  22.1 us (19%)
  waiting for transfers between devices  14.8 us (13%)
    all_to_all x1, blocking collectives, all_to_all(): lax.all_to_all(x, MODES, split_axis=0, concat_axis=0, tiled=True)  17 us
    all_to_all x1, blocking collectives, total_sum(): lax.all_to_all(x, 'mesh_1', split_axis=0, concat_axis=0, tiled=True)  17 us
    all_to_all x1, blocking collectives, total_sum(): lax.all_to_all(x, layer_axes, split_axis=0, concat_axis=0, tiled=True)  15 us
    all_to_all x2, starting transfers between devices, all_to_all(): lax.all_to_all(x, MODES, split_axis=0, concat_axis=0, tiled=True)  14.5 us
    all_to_all x2, waiting for transfers between devices, all_to_all(): lax.all_to_all(x, MODES, split_axis=0, concat_axis=0, tiled=True)  11.7 us
    pallas_call x1, Pallas kernels, per_device(): pl.pallas_call(stiffness_kernel, in_specs=[VMEM] * 5 + [SMEM], out_specs=...  10.8 us
    pallas_call x1, Pallas kernels, per_device(): pl.pallas_call(functools.partial(residual_kernel, total_dofs), in_specs=[...  7.94 us
    ppermute x3, starting transfers between devices, shifted(): return lax.ppermute(x, axis, pairs)  7.49 us
  transfers between devices with their start and end apart: 6, of which 3 were waited for; matrix products, arithmetic and copies ran while one was open for 0% of the time, Pallas kernels for 13%

profile of v1, /device:TPU:32, one launch (start us, length us, event | category | flops | bytes accessed | tf_op | source)
XLA Modules:
  0.0 113.3 jit_solution(3607861272305266576)
XLA Ops:
  0.6 1.9 %collective-permute-start = (f32[1728,128]{1,0:T(8,128)}, f32[1728,128]{1,0:T(8,128)S(1)}, u32[]{:S(2)}, u32[]{:S(2)}) collective-permute-start(f32[1728,128]{1,0:T(8,128)} %bitcast.16), channel_id=1, source_target_pairs={{0,8},{8,16},{16,24},{24,32},{32,40},{40,48},{48,56},{56,64},{64,7... | collective-permute-start | bytes 2654216 | tf_op jit(solution)/shard_map/ppermute | solution.py:29
  2.6 3.6 %collective-permute-start.1 = (f32[1728,128]{1,0:T(8,128)}, f32[1728,128]{1,0:T(8,128)S(1)}, u32[]{:S(2)}, u32[]{:S(2)}) collective-permute-start(f32[1728,128]{1,0:T(8,128)} %bitcast.17), channel_id=1, source_target_pairs={{8,0},{16,8},{24,16},{32,24},{40,32},{48,40},{56,48},{64,56},{72,6... | collective-permute-start | bytes 2654216 | tf_op jit(solution)/shard_map/ppermute | solution.py:29
  6.2 2.3 %split.1 = f32[1728,128]{1,0:T(8,128)} custom-call(f32[8,3,72,128]{3,2,1,0:T(8,128)} %bitcast.18), custom_call_target="tpu_custom_call" | custom-call | flops 100000 | bytes 1800000 | tf_op jit(solution)/shard_map/split/pallas_call | solution.py:409
  8.6 0.0 copy-start
  8.6 7.1 %all-to-all-start = ((f32[8,216,128]{2,1,0:T(8,128)}), f32[8,216,128]{2,1,0:T(8,128)S(1)}, u32[]{:S(2)}, u32[]{:S(2)}) async-start(f32[8,216,128]{2,1,0:T(8,128)} %bitcast.1), calls=%async_computation | async-start | bytes 1769472 | tf_op jit(solution)/shard_map/all_to_all | solution.py:413
  15.7 1.9 %collective-permute-start.2 = (s32[72,128]{1,0:T(8,128)}, s32[72,128]{1,0:T(8,128)S(1)}, u32[]{:S(2)}, u32[]{:S(2)}) collective-permute-start(s32[72,128]{1,0:T(8,128)} %bitcast.21), channel_id=1, source_target_pairs={{8,0},{16,8},{24,16},{32,24},{40,32},{48,40},{56,48},{64,56},{72,6... | collective-permute-start | bytes 110600 | tf_op jit(solution)/shard_map/ppermute | solution.py:29
  17.6 1.9 %collective-permute-done.2.classes_up = s32[72,128]{1,0:T(8,128)S(1)} collective-permute-done((s32[72,128]{1,0:T(8,128)}, s32[72,128]{1,0:T(8,128)S(1)}, u32[]{:S(2)}, u32[]{:S(2)}) %collective-permute-start.2) | collective-permute-done | bytes 36896 | tf_op jit(solution)/shard_map/ppermute | solution.py:29
  19.5 0.0 collective-permute-done.below
  19.5 0.0 collective-permute-done.1.above
  19.5 0.0 copy-start.1
  19.5 0.8 copy-done.1
  20.3 10.8 %stiffness.1 = f32[1728,128]{1,0:T(8,128)} custom-call(f32[1728,128]{1,0:T(8,128)S(1)} %bitcast.19, f32[1728,128]{1,0:T(8,128)S(1)} %collective-permute-done.below, f32[1728,128]{1,0:T(8,128)S(1)} %collective-permute-done.1.above, s32[72,128]{1,0:T(8,128)S(1)} %bitcast.22, s32[72,128]{1,0:T(8,128)S(1)} %collective-permute-done.2.classes_up, f32[16]{0:T(128)S(1)} %copy-done.3), custom_call_target="tpu_custom_call" | custom-call | flops 27000000 | bytes 3600000 | tf_op jit(solution)/shard_map/stiffness/pallas_call | solution.py:416
  31.1 0.0 all-to-all-done
  31.1 7.5 %all-to-all-start.1 = ((f32[8,216,128]{2,1,0:T(8,128)}), f32[8,216,128]{2,1,0:T(8,128)S(1)}, u32[]{:S(2)}, u32[]{:S(2)}) async-start(f32[8,216,128]{2,1,0:T(8,128)} %bitcast.5), calls=%async_computation.1 | async-start | bytes 1769472 | tf_op jit(solution)/shard_map/all_to_all | solution.py:413
  38.6 2.1 %mass.1 = (f32[64,64]{1,0:T(8,128)S(1)}, f32[16,128]{1,0:T(8,128)S(1)}) custom-call(f32[1728,128]{1,0:T(8,128)S(1)} %bitcast.10, s32[72,128]{1,0:T(8,128)S(1)} %bitcast.23, f32[16]{0:T(128)S(1)} %copy-done.3), custom_call_target="tpu_custom_call" | custom-call | flops 100000000 | bytes 900000 | tf_op jit(solution)/shard_map/mass/pallas_call | solution.py:430
  40.6 11.7 %all-to-all-done.1 = f32[8,216,128]{2,1,0:T(8,128)S(1)} async-done(((f32[8,216,128]{2,1,0:T(8,128)}), f32[8,216,128]{2,1,0:T(8,128)S(1)}, u32[]{:S(2)}, u32[]{:S(2)}) %all-to-all-start.1) | async-done | bytes 884768 | tf_op jit(solution)/shard_map/all_to_all | solution.py:413
  52.4 1.6 %grams.1 = f32[16,40,128]{2,1,0:T(8,128)S(1)} custom-call(f32[1728,128]{1,0:T(8,128)S(1)} %bitcast.11, f32[1728,128]{1,0:T(8,128)S(1)} %bitcast.13, f32[64,64]{1,0:T(8,128)S(1)} %get-tuple-element.6.mass), custom_call_target="tpu_custom_call" | custom-call | tf_op jit(solution)/shard_map/grams/pallas_call | solution.py:440
  54.0 15.0 %all_to_all.25 = f32[16,40,128]{2,1,0:T(8,128)S(1)} all-to-all(f32[16,40,128]{2,1,0:T(8,128)S(1)} %grams.1), channel_id=1, replica_groups=mesh['mesh_0'=2,'mesh_1'=8,'mesh_2'=2,'modes_0'=2,'modes_1'=4] {'mesh_0'..., dimensions={0} | all-to-all | bytes 655360 | tf_op jit(solution)/shard_map/all_to_all | solution.py:381
  69.0 0.1 collective-permute-start.3
  69.1 1.2 %collective-permute-done.3 = f32[40,128]{1,0:T(8,128)S(1)} collective-permute-done((f32[40,128]{1,0:T(8,128)S(1)}, f32[40,128]{1,0:T(8,128)S(1)}, u32[]{:S(2)}, u32[]{:S(2)}) %collective-permute-start.3) | collective-permute-done | bytes 20512 | tf_op jit(solution)/shard_map/ppermute | solution.py:382
  70.3 17.0 %all_to_all.26 = f32[8,40,128]{2,1,0:T(8,128)S(1)} all-to-all(f32[8,40,128]{2,1,0:T(8,128)S(1)} %broadcast_in_dim.2), channel_id=1, replica_groups=mesh['mesh_0'=2,'mesh_1'=8,'mesh_2'=2,'modes_0'=2,'modes_1'=4] {'mesh_1'}, dimensions={0} | all-to-all | bytes 327680 | tf_op jit(solution)/shard_map/all_to_all | solution.py:384
  87.3 7.9 %residual.1 = (f32[1728,128]{1,0:T(8,128)S(1)}, f32[64,64]{1,0:T(8,128)}) custom-call(f32[40,128]{1,0:T(8,128)S(1)} %reduce_sum.19.gram, f32[1728,128]{1,0:T(8,128)S(1)} %bitcast.12, f32[1728,128]{1,0:T(8,128)S(1)} %bitcast.14, f32[16,128]{1,0:T(8,128)S(1)} %get-tuple-element.7.density), custom_call_target="tpu_custom_call" | custom-call | tf_op jit(solution)/shard_map/residual/pallas_call | solution.py:449
  95.2 17.0 %all_to_all.27 = f32[8,216,128]{2,1,0:T(8,128)S(1)} all-to-all(f32[8,216,128]{2,1,0:T(8,128)S(1)} %bitcast.20), channel_id=1, replica_groups=mesh['mesh_0'=2,'mesh_1'=8,'mesh_2'=2,'modes_0'=2,'modes_1'=4] {'modes_0..., dimensions={0} | all-to-all | bytes 1769472 | tf_op jit(solution)/shard_map/all_to_all | solution.py:413
  112.2 1.1 join.1
  (9 shorter events, 0.1 us)
Async XLA Ops:
  0.6 18.9 %collective-permute-start = (f32[1728,128]{1,0:T(8,128)}, f32[1728,128]{1,0:T(8,128)S(1)}, u32[]{:S(2)}, u32[]{:S(2)}) collective-permute-start(f32[1728,128]{1,0:T(8,128)} %bitcast.16), channel_id=1, source_target_pairs={{0,8},{8,16},{16,24},{24,32},{32,40},{40,48},{48,56},{56,64},{64,7... | collective-permute-start | bytes 2654216 | tf_op jit(solution)/shard_map/ppermute | solution.py:29
  2.6 17.0 %collective-permute-start.1 = (f32[1728,128]{1,0:T(8,128)}, f32[1728,128]{1,0:T(8,128)S(1)}, u32[]{:S(2)}, u32[]{:S(2)}) collective-permute-start(f32[1728,128]{1,0:T(8,128)} %bitcast.17), channel_id=1, source_target_pairs={{8,0},{16,8},{24,16},{32,24},{40,32},{48,40},{56,48},{64,56},{72,6... | collective-permute-start | bytes 2654216 | tf_op jit(solution)/shard_map/ppermute | solution.py:29
  8.6 11.0 %copy-start = (f32[8,3,1,9216]{3,2,1,0:T(1,128)S(1)}, f32[8,3,1,9216]{3,2,1,0:T(1,128)}, u32[]{:S(2)}) copy-start(f32[8,3,1,9216]{3,2,1,0:T(1,128)} %param.3) | copy-start | bytes 2654212
  8.6 22.5 %all-to-all-start = ((f32[8,216,128]{2,1,0:T(8,128)}), f32[8,216,128]{2,1,0:T(8,128)S(1)}, u32[]{:S(2)}, u32[]{:S(2)}) async-start(f32[8,216,128]{2,1,0:T(8,128)} %bitcast.1), calls=%async_computation | async-start | bytes 1769472 | tf_op jit(solution)/shard_map/all_to_all | solution.py:413
  15.6 3.9 %copy-start.3 = (f32[16]{0:T(128)S(1)}, f32[16]{0:T(128)}, u32[]{:S(2)}) copy-start(f32[16]{0:T(128)} %levels.3) | copy-start | bytes 196
  15.7 3.9 %collective-permute-start.2 = (s32[72,128]{1,0:T(8,128)}, s32[72,128]{1,0:T(8,128)S(1)}, u32[]{:S(2)}, u32[]{:S(2)}) collective-permute-start(s32[72,128]{1,0:T(8,128)} %bitcast.21), channel_id=1, source_target_pairs={{8,0},{16,8},{24,16},{32,24},{40,32},{48,40},{56,48},{64,56},{72,6... | collective-permute-start | bytes 110600 | tf_op jit(solution)/shard_map/ppermute | solution.py:29
  19.5 0.8 copy-start.1
  31.1 7.5 %copy-start.2 = (s32[1,9216]{1,0:T(1,128)S(1)}, s32[1,9216]{1,0:T(1,128)}, u32[]{:S(2)}) copy-start(s32[1,9216]{1,0:T(1,128)} %param.4) | copy-start | bytes 110596
  31.1 21.3 %all-to-all-start.1 = ((f32[8,216,128]{2,1,0:T(8,128)}), f32[8,216,128]{2,1,0:T(8,128)S(1)}, u32[]{:S(2)}, u32[]{:S(2)}) async-start(f32[8,216,128]{2,1,0:T(8,128)} %bitcast.5), calls=%async_computation.1 | async-start | bytes 1769472 | tf_op jit(solution)/shard_map/all_to_all | solution.py:413
  69.0 1.3 %collective-permute-start.3 = (f32[40,128]{1,0:T(8,128)S(1)}, f32[40,128]{1,0:T(8,128)S(1)}, u32[]{:S(2)}, u32[]{:S(2)}) collective-permute-start(f32[40,128]{1,0:T(8,128)S(1)} %reduce_sum.18), channel_id=1, source_target_pairs={{0,8},{8,0},{1,9},{9,1},{2,10},{10,2},{3,11},{11,3},{4,12},{12,4},... | collective-permute-start | bytes 61448 | tf_op jit(solution)/shard_map/ppermute | solution.py:382

commit v2 on v1

--- a/solution.py
+++ b/solution.py
@@ -18,6 +18,7 @@
 
 highest = lax.Precision.HIGHEST
 floor_modulus = 0.001
+AHEAD = 2
 VMEM = pl.BlockSpec(memory_space=pltpu.VMEM)
 SMEM = pl.BlockSpec(memory_space=pltpu.SMEM)
 HBM = pl.BlockSpec(memory_space=pltpu.HBM)
@@ -157,7 +158,8 @@
 
 
 def stiffness_kernel(
-    own, below, above, classes, classes_up, levels, out, low, high, even_buf, odd_buf, sums, ends
+    own, below, above, classes, classes_up, levels, out, low, high,
+    runs, x_fields, turned, forces, sums,
 ):
     low[...] = UNIT * modulus_of(densities(classes[...], levels))
     is_top = lax.axis_index(MESH) == lax.axis_size(MESH) - 1
@@ -167,96 +169,105 @@
     before_end = (lane != 95, lane != 63, (lane != 31) & (lane != 127))
     planes = (own, below, above)
 
-    def forward(g, buf):
+    def fetch(h, k):
         for p in range(3):
             for c in range(3):
-                s = p * 3 + c
-                old = sums[2 * s], sums[2 * s + 1]
-                runs = [planes[p][pl.ds(c * 72 + 3 * g + k, 8, stride=216), :] for k in range(3)]
-                rolled = [pltpu.roll(u, 1, 1) for u in runs]
-                for k in range(3):
-                    back = jnp.where(inside[k], rolled[k], 0.0)
-                    if k:
-                        back = jnp.where(lane == 0, rolled[k - 1], back)
-                    total, diff = runs[k] + back, runs[k] - back
-                    new = pltpu.roll(total, 96, 1), pltpu.roll(diff, 96, 1)
-                    row_total = jnp.where(lane < 96, old[0], new[0])
-                    row_diff = jnp.where(lane < 96, old[1], new[1])
-                    old = new
-                    base = k * 36 + s * 4
-                    buf[base] = total + row_total
-                    buf[base + 1] = diff + row_diff
-                    buf[base + 2] = total - row_total
-                    buf[base + 3] = diff - row_diff
-                sums[2 * s], sums[2 * s + 1] = old
-
-    def store(run, c, value):
-        row = lax.div(run, 9) * 216 + lax.rem(run, 9) + c * 9
-        out[pl.ds(row, 8, stride=27), :] = value
-
-    def inverse(g, buf):
-        kept, moved = [], []
-        for k in range(3):
-            own_f, below_f, above_f = [
-                {
-                    (c, name): buf[k * 36 + (p * 3 + c) * 4 + n]
-                    for c in range(3)
-                    for n, name in enumerate(PARITIES)
-                }
-                for p in range(3)
-            ]
-            even, odd = layer(own_f, below_f)
-            even_up, odd_up = layer(above_f, own_f)
-            weight = jnp.broadcast_to(low[pl.ds(3 * g + k, 1), :], (8, LANES))
-            weight_up = jnp.broadcast_to(high[pl.ds(3 * g + k, 1), :], (8, LANES))
-            keep, move = [], []
+                u = planes[p][pl.ds(c * 72 + 6 * h + k, 8, stride=216), :]
+                runs[(p * 3 + c) * 6 + k] = u
+                runs[54 + (p * 3 + c) * 6 + k] = pltpu.roll(u, 1, 1)
+
+    def along_x(k):
+        for s in range(9):
+            u, rolled = runs[s * 6 + k], runs[54 + s * 6 + k]
+            back = jnp.where(inside[k % 3], rolled, 0.0)
+            if k % 3:
+                back = jnp.where(lane == 0, runs[54 + s * 6 + k - 1], back)
+            for n, v in enumerate((u + back, u - back)):
+                x_fields[n * 63 + s * 7 + k + 1] = v
+                turned[n * 63 + s * 7 + k + 1] = pltpu.roll(v, 96, 1)
+
+    def element_forces(h, k):
+        own_f, below_f, above_f = {}, {}, {}
+        for p, group in enumerate((own_f, below_f, above_f)):
             for c in range(3):
-                f = {"00": weight * odd[c, "00"] - weight_up * odd_up[c, "00"]}
-                for n in PARITIES[1:]:
-                    f[n] = weight * (even[c, n] + odd[c, n]) + weight_up * (
-                        even_up[c, n] - odd_up[c, n]
-                    )
-                keep.append((f["00"] + f["10"], f["01"] + f["11"]))
-                move.append(
-                    [pltpu.roll(v, 127, 1) for v in (f["00"] - f["10"], f["01"] - f["11"])]
+                for n, name in enumerate("01"):
+                    at = n * 63 + (p * 3 + c) * 7 + k
+                    row = jnp.where(lane < 96, turned[at], turned[at + 1])
+                    here = x_fields[at + 1]
+                    group[c, name + "0"] = here + row
+                    group[c, name + "1"] = here - row
+        even, odd = layer(own_f, below_f)
+        even_up, odd_up = layer(above_f, own_f)
+        weight = jnp.broadcast_to(low[pl.ds(6 * h + k, 1), :], (8, LANES))
+        weight_up = jnp.broadcast_to(high[pl.ds(6 * h + k, 1), :], (8, LANES))
+        for c in range(3):
+            f = {"00": weight * odd[c, "00"] - weight_up * odd_up[c, "00"]}
+            for n in PARITIES[1:]:
+                f[n] = weight * (even[c, n] + odd[c, n]) + weight_up * (
+                    even_up[c, n] - odd_up[c, n]
                 )
-            kept.append(keep)
-            moved.append(move)
+            base = k * 12 + c * 4
+            forces[base] = f["00"] + f["10"]
+            forces[base + 1] = f["01"] + f["11"]
+            forces[base + 2] = pltpu.roll(f["00"] - f["10"], 127, 1)
+            forces[base + 3] = pltpu.roll(f["01"] - f["11"], 127, 1)
+        if k == 5:
+            for at in range(0, 126, 7):
+                turned[at] = turned[at + 6]
+
+    def gather_x(k):
         for c in range(3):
-            old_plus, old_minus = ends[2 * c], ends[2 * c + 1]
-            for k in range(3):
-                pair = []
-                for y in range(2):
-                    from_right = jnp.where(before_end[k], moved[k][c][y], 0.0)
-                    if k < 2:
-                        from_right = jnp.where(lane == 127, moved[k + 1][c][y], from_right)
-                    pair.append(kept[k][c][y] + from_right)
-                plus, minus = pair[0] + pair[1], pltpu.roll(pair[0] - pair[1], 32, 1)
-                store(
-                    jnp.maximum(3 * g + k - 1, 0),
-                    c,
-                    old_plus + jnp.where(lane < 32, old_minus, minus),
-                )
-                old_plus, old_minus = plus, minus
-            ends[2 * c], ends[2 * c + 1] = old_plus, old_minus
+            pair = []
+            for y in range(2):
+                base = k * 12 + c * 4 + y
+                from_right = jnp.where(before_end[k % 3], forces[base + 2], 0.0)
+                if k % 3 < 2:
+                    from_right = jnp.where(lane == 127, forces[base + 14], from_right)
+                pair.append(forces[base] + from_right)
+            sums[c * 7 + k + 1] = pair[0] + pair[1]
+            sums[21 + c * 7 + k + 1] = pltpu.roll(pair[0] - pair[1], 32, 1)
+
+    def gather_y(h, k):
+        run = jnp.maximum(6 * h + k - 1, 0)
+        row = lax.div(run, 9) * 216 + lax.rem(run, 9)
+        for c in range(3):
+            at = c * 7 + k
+            turned_back = jnp.where(lane < 32, sums[21 + at], sums[22 + at])
+            out[pl.ds(row + c * 9, 8, stride=27), :] = sums[at] + turned_back
+        if k == 5:
+            for at in range(0, 42, 7):
+                sums[at] = sums[at + 6]
 
     zero = jnp.zeros((8, LANES), jnp.float32)
-    for k in range(18):
-        sums[k] = zero
-    for k in range(6):
-        ends[k] = zero
-    forward(0, even_buf)
-
-    def two_groups(h, carry):
-        forward(2 * h + 1, odd_buf)
-        inverse(2 * h, even_buf)
-        forward(jnp.minimum(2 * h + 2, 23), even_buf)
-        inverse(2 * h + 1, odd_buf)
+    for at in range(0, 126, 7):
+        turned[at] = zero
+    for at in range(0, 42, 7):
+        sums[at] = zero
+
+    def step(t, carry=None):
+        fixed = isinstance(t, int)
+        stages = (
+            (0, 4, 16, lambda k: gather_y(t - 4, k)),
+            (1, 3, 15, gather_x),
+            (1, 2, 14, lambda k: element_forces(t - 2, k)),
+            (2, 1, 13, along_x),
+            (3, 0, 12, lambda k: fetch(t, k)),
+        )
+        for turn in range(9):
+            for delay, start, end, stage in stages:
+                if 0 <= turn - delay < 6 and (not fixed or start <= t < end):
+                    stage(turn - delay)
         return carry
 
-    lax.fori_loop(0, 12, two_groups, 0)
+    for t in range(4):
+        step(t)
+    lax.fori_loop(4, 12, step, 0)
+    for t in range(12, 16):
+        step(t)
     for c in range(3):
-        store(71, c, ends[2 * c] + jnp.where(lane < 32, ends[2 * c + 1], 0.0))
+        out[pl.ds(7 * 216 + 8 + c * 9, 8, stride=27), :] = sums[c * 7] + jnp.where(
+            lane < 32, sums[21 + c * 7], 0.0
+        )
 
 
 def mass_kernel(basis, classes, levels, mass, band_density, density):
@@ -313,19 +324,47 @@
 def inverse_factor(mass):
     row = lax.broadcasted_iota(jnp.int32, (64, LANES), 0)
     lane = lax.broadcasted_iota(jnp.int32, (64, LANES), 1)
-    w = jnp.where(
+    start = jnp.where(
         lane < 64,
         jnp.concatenate([mass, mass], 1),
         jnp.where(lane - 64 == row, 1.0, 0.0),
     )
-    for k in range(0, 64, 2):
-        r0, r1 = w[k : k + 1, :], w[k + 1 : k + 2, :]
-        c0, c1 = w[:, k : k + 1], w[:, k + 1 : k + 2]
-        a, b, d = r0[:, k : k + 1], r0[:, k + 1 : k + 2], r1[:, k + 1 : k + 2]
+    w = [start[8 * i : 8 * i + 8] for i in range(8)]
+    row_in_block = lax.broadcasted_iota(jnp.int32, (8, LANES), 0)
+
+    def spread(pair):
+        return [
+            {
+                i: jnp.broadcast_to(w[i][:, k : k + 1], (8, LANES))
+                for i in range(2 * pair // 8, 8)
+            }
+            for k in (2 * pair, 2 * pair + 1)
+        ]
+
+    def at(column, k):
+        return column[k // 8][k % 8 : k % 8 + 1]
+
+    waiting = {pair: spread(pair) for pair in range(AHEAD)}
+    for pair in range(32):
+        if pair + AHEAD < 32:
+            waiting[pair + AHEAD] = spread(pair + AHEAD)
+        c0, c1 = waiting.pop(pair)
+        k = 2 * pair
+        a, b, d = at(c0, k), at(c0, k + 1), at(c1, k + 1)
         inv = 1.0 / (a * d - b * b)
-        x0 = (d * r0 - b * r1) * inv
-        x1 = (a * r1 - b * r0) * inv
-        w = jnp.where(row > k + 1, w - c0 * x0 - c1 * x1, w)
+        da, db, dd = a * inv, b * inv, d * inv
+        for later, columns in waiting.items():
+            for n, column in enumerate(columns):
+                p0, p1 = at(c0, 2 * later + n), at(c1, 2 * later + n)
+                y0, y1 = dd * p0 - db * p1, da * p1 - db * p0
+                for i in column:
+                    column[i] = column[i] - c0[i] * y0 - c1[i] * y1
+        r0, r1 = at(w, k), at(w, k + 1)
+        x0, x1 = dd * r0 - db * r1, da * r1 - db * r0
+        for i in range((k + 2) // 8, 8):
+            new = w[i] - c0[i] * x0 - c1[i] * x1
+            w[i] = jnp.where(row_in_block + 8 * i > k + 1, new, w[i]) if 8 * i < k + 2 else new
+    w = jnp.concatenate(w, 0)
     diagonal = jnp.sum(jnp.where(lane == row, w, 0.0), 1, keepdims=True)
     left = jnp.sum(jnp.where(lane == row - 1, w, 0.0), 1, keepdims=True)
     odd = row % 2 == 1
@@ -419,7 +458,7 @@
         out_specs=VMEM,
         out_shape=f32(1728, LANES),
         scratch_shapes=[pltpu.VMEM((72, LANES), jnp.float32)] * 2
-        + [pltpu.VMEM((n, 8, LANES), jnp.float32) for n in (108, 108, 18, 6)],
+        + [pltpu.VMEM((n, 8, LANES), jnp.float32) for n in (108, 126, 126, 72, 42)],
         compiler_params=room(12),
         cost_estimate=pl.CostEstimate(
             flops=27_000_000, bytes_accessed=3_600_000, transcendentals=0

time: 115 us -> 107 us (0.930)
  Pallas kernels: 25.8 us -> 17.8 us
  waiting for transfers between devices: 14.8 us -> 18.2 us
  starting transfers between devices: 22.1 us -> 18.9 us
    pallas_call x1, Pallas kernels: 10.8 us -> 6.59 us  [per_device(): pl.pallas_call(stiffness_kernel, in_specs=[VMEM] * 5 + [SMEM], out_specs=...]
    pallas_call x1, Pallas kernels: 7.94 us -> 4.09 us  [per_device(): pl.pallas_call(functools.partial(residual_kernel, total_dofs), in_specs=[...]
    all_to_all x2, waiting for transfers between devices: 11.7 us -> 15.1 us  [all_to_all(): lax.all_to_all(x, MODES, split_axis=0, concat_axis=0, tiled=True)]
    all_to_all x2, starting transfers between devices: 14.5 us -> 11.3 us  [all_to_all(): lax.all_to_all(x, MODES, split_axis=0, concat_axis=0, tiled=True)]
  transfers between devices with their start and end apart: 6 -> 6, of which waited for: 3 -> 4; matrix products, arithmetic and copies ran while one was open for 0% -> 0% of each run, Pallas kernels for 13% -> 10%
where the time goes in v2:
time: 107 us; the launch traced here: 105 us
  blocking collectives  48.9 us (46%)
  starting transfers between devices  18.9 us (18%)
  waiting for transfers between devices  18.2 us (17%)
  Pallas kernels  17.8 us (17%)
    all_to_all x1, blocking collectives, all_to_all(): lax.all_to_all(x, MODES, split_axis=0, concat_axis=0, tiled=True)  17 us
    all_to_all x1, blocking collectives, total_sum(): lax.all_to_all(x, 'mesh_1', split_axis=0, concat_axis=0, tiled=True)  16.9 us
    all_to_all x2, waiting for transfers between devices, all_to_all(): lax.all_to_all(x, MODES, split_axis=0, concat_axis=0, tiled=True)  15.1 us
    all_to_all x1, blocking collectives, total_sum(): lax.all_to_all(x, layer_axes, split_axis=0, concat_axis=0, tiled=True)  15 us
    all_to_all x2, starting transfers between devices, all_to_all(): lax.all_to_all(x, MODES, split_axis=0, concat_axis=0, tiled=True)  11.3 us
    ppermute x3, starting transfers between devices, shifted(): return lax.ppermute(x, axis, pairs)  7.49 us
    pallas_call x1, Pallas kernels, per_device(): pl.pallas_call(stiffness_kernel, in_specs=[VMEM] * 5 + [SMEM], out_specs=...  6.59 us
    pallas_call x1, Pallas kernels, per_device(): pl.pallas_call(functools.partial(residual_kernel, total_dofs), in_specs=[...  4.09 us
  transfers between devices with their start and end apart: 6, of which 4 were waited for; matrix products, arithmetic and copies ran while one was open for 0% of the time, Pallas kernels for 10%

profile of v2, /device:TPU:32, one launch (start us, length us, event | category | flops | bytes accessed | tf_op | source)
XLA Modules:
  0.0 105.3 jit_solution(12181639679365722501)
XLA Ops:
  0.6 1.9 %collective-permute-start = (f32[1728,128]{1,0:T(8,128)}, f32[1728,128]{1,0:T(8,128)S(1)}, u32[]{:S(2)}, u32[]{:S(2)}) collective-permute-start(f32[1728,128]{1,0:T(8,128)} %bitcast.16), channel_id=1, source_target_pairs={{0,8},{8,16},{16,24},{24,32},{32,40},{40,48},{48,56},{56,64},{64,7... | collective-permute-start | bytes 2654216 | tf_op jit(solution)/shard_map/ppermute | solution.py:30
  2.6 3.6 %collective-permute-start.1 = (f32[1728,128]{1,0:T(8,128)}, f32[1728,128]{1,0:T(8,128)S(1)}, u32[]{:S(2)}, u32[]{:S(2)}) collective-permute-start(f32[1728,128]{1,0:T(8,128)} %bitcast.17), channel_id=1, source_target_pairs={{8,0},{16,8},{24,16},{32,24},{40,32},{48,40},{56,48},{64,56},{72,6... | collective-permute-start | bytes 2654216 | tf_op jit(solution)/shard_map/ppermute | solution.py:30
  6.2 2.3 %split.1 = f32[1728,128]{1,0:T(8,128)} custom-call(f32[8,3,72,128]{3,2,1,0:T(8,128)} %bitcast.18), custom_call_target="tpu_custom_call" | custom-call | flops 100000 | bytes 1800000 | tf_op jit(solution)/shard_map/split/pallas_call | solution.py:448
  8.6 0.0 copy-start
  8.6 7.1 %all-to-all-start = ((f32[8,216,128]{2,1,0:T(8,128)}), f32[8,216,128]{2,1,0:T(8,128)S(1)}, u32[]{:S(2)}, u32[]{:S(2)}) async-start(f32[8,216,128]{2,1,0:T(8,128)} %bitcast.1), calls=%async_computation | async-start | bytes 1769472 | tf_op jit(solution)/shard_map/all_to_all | solution.py:452
  15.7 1.9 %collective-permute-start.2 = (s32[72,128]{1,0:T(8,128)}, s32[72,128]{1,0:T(8,128)S(1)}, u32[]{:S(2)}, u32[]{:S(2)}) collective-permute-start(s32[72,128]{1,0:T(8,128)} %bitcast.21), channel_id=1, source_target_pairs={{8,0},{16,8},{24,16},{32,24},{40,32},{48,40},{56,48},{64,56},{72,6... | collective-permute-start | bytes 110600 | tf_op jit(solution)/shard_map/ppermute | solution.py:30
  17.6 1.9 %collective-permute-done.2.classes_up = s32[72,128]{1,0:T(8,128)S(1)} collective-permute-done((s32[72,128]{1,0:T(8,128)}, s32[72,128]{1,0:T(8,128)S(1)}, u32[]{:S(2)}, u32[]{:S(2)}) %collective-permute-start.2) | collective-permute-done | bytes 36896 | tf_op jit(solution)/shard_map/ppermute | solution.py:30
  19.5 0.0 collective-permute-done.below
  19.5 0.0 collective-permute-done.1.above
  19.5 0.0 copy-start.1
  19.5 0.8 copy-done.1
  20.3 6.6 %stiffness.1 = f32[1728,128]{1,0:T(8,128)} custom-call(f32[1728,128]{1,0:T(8,128)S(1)} %bitcast.19, f32[1728,128]{1,0:T(8,128)S(1)} %collective-permute-done.below, f32[1728,128]{1,0:T(8,128)S(1)} %collective-permute-done.1.above, s32[72,128]{1,0:T(8,128)S(1)} %bitcast.22, s32[72,128]{1,0:T(8,128)S(1)} %collective-permute-done.2.classes_up, f32[16]{0:T(128)S(1)} %copy-done.3), custom_call_target="tpu_custom_call" | custom-call | flops 27000000 | bytes 3600000 | tf_op jit(solution)/shard_map/stiffness/pallas_call | solution.py:455
  26.9 3.3 %all-to-all-done = f32[8,216,128]{2,1,0:T(8,128)S(1)} async-done(((f32[8,216,128]{2,1,0:T(8,128)}), f32[8,216,128]{2,1,0:T(8,128)S(1)}, u32[]{:S(2)}, u32[]{:S(2)}) %all-to-all-start) | async-done | bytes 884768 | tf_op jit(solution)/shard_map/all_to_all | solution.py:452
  30.2 4.2 %all-to-all-start.1 = ((f32[8,216,128]{2,1,0:T(8,128)}), f32[8,216,128]{2,1,0:T(8,128)S(1)}, u32[]{:S(2)}, u32[]{:S(2)}) async-start(f32[8,216,128]{2,1,0:T(8,128)} %bitcast.5), calls=%async_computation.1 | async-start | bytes 1769472 | tf_op jit(solution)/shard_map/all_to_all | solution.py:452
  34.4 2.1 %mass.1 = (f32[64,64]{1,0:T(8,128)S(1)}, f32[16,128]{1,0:T(8,128)S(1)}) custom-call(f32[1728,128]{1,0:T(8,128)S(1)} %bitcast.10, s32[72,128]{1,0:T(8,128)S(1)} %bitcast.23, f32[16]{0:T(128)S(1)} %copy-done.3), custom_call_target="tpu_custom_call" | custom-call | flops 100000000 | bytes 900000 | tf_op jit(solution)/shard_map/mass/pallas_call | solution.py:469
  36.5 11.8 %all-to-all-done.1 = f32[8,216,128]{2,1,0:T(8,128)S(1)} async-done(((f32[8,216,128]{2,1,0:T(8,128)}), f32[8,216,128]{2,1,0:T(8,128)S(1)}, u32[]{:S(2)}, u32[]{:S(2)}) %all-to-all-start.1) | async-done | bytes 884768 | tf_op jit(solution)/shard_map/all_to_all | solution.py:452
  48.3 1.6 %grams.1 = f32[16,40,128]{2,1,0:T(8,128)S(1)} custom-call(f32[1728,128]{1,0:T(8,128)S(1)} %bitcast.11, f32[1728,128]{1,0:T(8,128)S(1)} %bitcast.13, f32[64,64]{1,0:T(8,128)S(1)} %get-tuple-element.6.mass), custom_call_target="tpu_custom_call" | custom-call | tf_op jit(solution)/shard_map/grams/pallas_call | solution.py:479
  49.9 15.0 %all_to_all.25 = f32[16,40,128]{2,1,0:T(8,128)S(1)} all-to-all(f32[16,40,128]{2,1,0:T(8,128)S(1)} %grams.1), channel_id=1, replica_groups=mesh['mesh_0'=2,'mesh_1'=8,'mesh_2'=2,'modes_0'=2,'modes_1'=4] {'mesh_0'..., dimensions={0} | all-to-all | bytes 655360 | tf_op jit(solution)/shard_map/all_to_all | solution.py:420
  64.9 0.1 collective-permute-start.3
  65.0 1.2 %collective-permute-done.3 = f32[40,128]{1,0:T(8,128)S(1)} collective-permute-done((f32[40,128]{1,0:T(8,128)S(1)}, f32[40,128]{1,0:T(8,128)S(1)}, u32[]{:S(2)}, u32[]{:S(2)}) %collective-permute-start.3) | collective-permute-done | bytes 20512 | tf_op jit(solution)/shard_map/ppermute | solution.py:421
  66.2 16.9 %all_to_all.26 = f32[8,40,128]{2,1,0:T(8,128)S(1)} all-to-all(f32[8,40,128]{2,1,0:T(8,128)S(1)} %broadcast_in_dim.2), channel_id=1, replica_groups=mesh['mesh_0'=2,'mesh_1'=8,'mesh_2'=2,'modes_0'=2,'modes_1'=4] {'mesh_1'}, dimensions={0} | all-to-all | bytes 327680 | tf_op jit(solution)/shard_map/all_to_all | solution.py:423
  83.1 4.1 %residual.1 = (f32[1728,128]{1,0:T(8,128)S(1)}, f32[64,64]{1,0:T(8,128)}) custom-call(f32[40,128]{1,0:T(8,128)S(1)} %reduce_sum.19.gram, f32[1728,128]{1,0:T(8,128)S(1)} %bitcast.12, f32[1728,128]{1,0:T(8,128)S(1)} %bitcast.14, f32[16,128]{1,0:T(8,128)S(1)} %get-tuple-element.7.density), custom_call_target="tpu_custom_call" | custom-call | tf_op jit(solution)/shard_map/residual/pallas_call | solution.py:488
  87.2 17.0 %all_to_all.27 = f32[8,216,128]{2,1,0:T(8,128)S(1)} all-to-all(f32[8,216,128]{2,1,0:T(8,128)S(1)} %bitcast.20), channel_id=1, replica_groups=mesh['mesh_0'=2,'mesh_1'=8,'mesh_2'=2,'modes_0'=2,'modes_1'=4] {'modes_0..., dimensions={0} | all-to-all | bytes 1769472 | tf_op jit(solution)/shard_map/all_to_all | solution.py:452
  104.2 1.1 %join.1 = f32[1728,128]{1,0:T(8,128)} custom-call(f32[1728,128]{1,0:T(8,128)S(1)} %bitcast.15), custom_call_target="tpu_custom_call" | custom-call | tf_op jit(solution)/shard_map/join/pallas_call | solution.py:496
  (9 shorter events, 0.1 us)
Async XLA Ops:
  0.6 18.9 %collective-permute-start = (f32[1728,128]{1,0:T(8,128)}, f32[1728,128]{1,0:T(8,128)S(1)}, u32[]{:S(2)}, u32[]{:S(2)}) collective-permute-start(f32[1728,128]{1,0:T(8,128)} %bitcast.16), channel_id=1, source_target_pairs={{0,8},{8,16},{16,24},{24,32},{32,40},{40,48},{48,56},{56,64},{64,7... | collective-permute-start | bytes 2654216 | tf_op jit(solution)/shard_map/ppermute | solution.py:30
  2.6 17.0 %collective-permute-start.1 = (f32[1728,128]{1,0:T(8,128)}, f32[1728,128]{1,0:T(8,128)S(1)}, u32[]{:S(2)}, u32[]{:S(2)}) collective-permute-start(f32[1728,128]{1,0:T(8,128)} %bitcast.17), channel_id=1, source_target_pairs={{8,0},{16,8},{24,16},{32,24},{40,32},{48,40},{56,48},{64,56},{72,6... | collective-permute-start | bytes 2654216 | tf_op jit(solution)/shard_map/ppermute | solution.py:30
  8.6 11.0 %copy-start = (f32[8,3,1,9216]{3,2,1,0:T(1,128)S(1)}, f32[8,3,1,9216]{3,2,1,0:T(1,128)}, u32[]{:S(2)}) copy-start(f32[8,3,1,9216]{3,2,1,0:T(1,128)} %param.3) | copy-start | bytes 2654212
  8.6 21.6 %all-to-all-start = ((f32[8,216,128]{2,1,0:T(8,128)}), f32[8,216,128]{2,1,0:T(8,128)S(1)}, u32[]{:S(2)}, u32[]{:S(2)}) async-start(f32[8,216,128]{2,1,0:T(8,128)} %bitcast.1), calls=%async_computation | async-start | bytes 1769472 | tf_op jit(solution)/shard_map/all_to_all | solution.py:452
  15.6 3.9 %copy-start.3 = (f32[16]{0:T(128)S(1)}, f32[16]{0:T(128)}, u32[]{:S(2)}) copy-start(f32[16]{0:T(128)} %levels.3) | copy-start | bytes 196
  15.7 3.9 %collective-permute-start.2 = (s32[72,128]{1,0:T(8,128)}, s32[72,128]{1,0:T(8,128)S(1)}, u32[]{:S(2)}, u32[]{:S(2)}) collective-permute-start(s32[72,128]{1,0:T(8,128)} %bitcast.21), channel_id=1, source_target_pairs={{8,0},{16,8},{24,16},{32,24},{40,32},{48,40},{56,48},{64,56},{72,6... | collective-permute-start | bytes 110600 | tf_op jit(solution)/shard_map/ppermute | solution.py:30
  19.5 0.8 copy-start.1
  30.2 4.2 %copy-start.2 = (s32[1,9216]{1,0:T(1,128)S(1)}, s32[1,9216]{1,0:T(1,128)}, u32[]{:S(2)}) copy-start(s32[1,9216]{1,0:T(1,128)} %param.4) | copy-start | bytes 110596
  30.2 18.1 %all-to-all-start.1 = ((f32[8,216,128]{2,1,0:T(8,128)}), f32[8,216,128]{2,1,0:T(8,128)S(1)}, u32[]{:S(2)}, u32[]{:S(2)}) async-start(f32[8,216,128]{2,1,0:T(8,128)} %bitcast.5), calls=%async_computation.1 | async-start | bytes 1769472 | tf_op jit(solution)/shard_map/all_to_all | solution.py:452
  64.9 1.3 %collective-permute-start.3 = (f32[40,128]{1,0:T(8,128)S(1)}, f32[40,128]{1,0:T(8,128)S(1)}, u32[]{:S(2)}, u32[]{:S(2)}) collective-permute-start(f32[40,128]{1,0:T(8,128)S(1)} %reduce_sum.18), channel_id=1, source_target_pairs={{0,8},{8,0},{1,9},{9,1},{2,10},{10,2},{3,11},{11,3},{4,12},{12,4},... | collective-permute-start | bytes 61448 | tf_op jit(solution)/shard_map/ppermute | solution.py:421

commit v3 on v2

--- a/solution.py
+++ b/solution.py
@@ -270,17 +270,15 @@
         )
 
 
-def mass_kernel(basis, classes, levels, mass, band_density, density):
+def halves(x):
+    high = x.astype(jnp.bfloat16)
+    return high, (x - high.astype(jnp.float32)).astype(jnp.bfloat16)
+
+
+def band_densities(classes, levels, density):
     density[...] = densities(classes[...], levels)
     band = lax.axis_index(MODES)
-    acc = jnp.zeros((64, 64), jnp.float32)
-    for q in range(9):
-        row = density[pl.ds(band * 9 + q, 1), :]
-        band_density[pl.ds(q, 1), :] = row
-        for c in range(3):
-            b = basis[pl.ds(c * 9 + q, 64, stride=27), :]
-            acc = acc + dot(b, b * row, ((1,), (1,)))
-    mass[...] = acc
+    return [density[pl.ds(band * 9 + q, 1), :] for q in range(9)]
 
 
 def square_index():
@@ -288,14 +286,26 @@
     return row, lax.broadcasted_iota(jnp.int32, (64, 64), 1)
 
 
-def gram_kernel(basis, image, mass, out):
-    acc = jnp.zeros((64, 64), jnp.float32)
-    for t in range(27):
-        b = basis[pl.ds(t, 64, stride=27), :]
-        v = image[pl.ds(t, 64, stride=27), :]
-        acc = acc + dot(b, v, ((1,), (1,)))
+def gram_kernel(basis, image, classes, levels, out, density):
+    rows = band_densities(classes, levels, density)
+    acc = jnp.zeros((64, LANES), jnp.float32)
+    for c in range(3):
+        left, right = [], []
+        for q in range(9):
+            b = basis[pl.ds(c * 9 + q, 64, stride=27), :]
+            v = image[pl.ds(c * 9 + q, 64, stride=27), :]
+            b_high, b_low = halves(b)
+            v_high, v_low = halves(jnp.concatenate([v, b * rows[q]], 0))
+            left += [b_high, b_low, b_high]
+            right += [v_high, v_high, v_low]
+        acc = acc + lax.dot_general(
+            jnp.concatenate(left, 1),
+            jnp.concatenate(right, 1),
+            (((1,), (1,)), ((), ())),
+            preferred_element_type=jnp.float32,
+        )
+    acc, mass = acc[:, :64], acc[:, 64:]
     row, column = square_index()
-    mass = mass[...]
     packed = jnp.where(row >= column, acc, mass)
     diagonal = jnp.sum(jnp.where(row == column, mass, 0.0), 0, keepdims=True)
     top = jnp.concatenate([packed[:32], packed[32:]], 1)
@@ -376,22 +386,26 @@
     return scaled[:, 64:]
 
 
-def residual_kernel(total_dofs, gram, basis, image, density, out, ritz_ref):
-    scale = 1.0 / total_dofs
-    stiff, mass = unpacked(gram[...] * scale)
+def residual_kernel(total_dofs, gram, basis, image, classes, levels, out, ritz_ref, density):
+    rows = band_densities(classes, levels, density)
+    stiff, mass = unpacked(gram[...] * (1.0 / total_dofs))
     inverse = inverse_factor(mass)
     ritz = dot(dot(inverse, stiff, ((1,), (0,))), inverse, ((1,), (1,)))
     ritz_ref[...] = ritz
     mixed = dot(ritz, inverse, ((0,), (0,)))
-    weights = jnp.concatenate([inverse, -mixed], 1)
-    for c in range(3):
-        for q in range(9):
+    high, low = halves(jnp.concatenate([inverse, -mixed], 1))
+    weights = jnp.concatenate([high, low, high], 1)
+    for q in range(9):
+        for c in range(3):
             t = c * 9 + q
             b = basis[pl.ds(t, 64, stride=27), :]
             v = image[pl.ds(t, 64, stride=27), :]
-            m = b * density[pl.ds(q, 1), :]
-            out[pl.ds(t, 64, stride=27), :] = dot(
-                weights, jnp.concatenate([v, m], 0), ((1,), (0,))
+            x_high, x_low = halves(jnp.concatenate([v, b * rows[q]], 0))
+            out[pl.ds(t, 64, stride=27), :] = lax.dot_general(
+                weights,
+                jnp.concatenate([x_high, x_high, x_low], 0),
+                (((1,), (0,)), ((), ())),
+                preferred_element_type=jnp.float32,
             )
 
 
@@ -464,35 +478,34 @@
             flops=27_000_000, bytes_accessed=3_600_000, transcendentals=0
         ),
         name="stiffness",
-    )(flat, below, above, classes, classes_up, level_density)
+    )(
+        pltpu.with_memory_space_constraint(flat, pltpu.HBM),
+        below,
+        above,
+        pltpu.with_memory_space_constraint(classes, pltpu.HBM),
+        classes_up,
+        level_density,
+    )
     image = all_to_all(image_pieces)
-    mass, band_density = pl.pallas_call(
-        mass_kernel,
-        in_specs=[VMEM, VMEM, SMEM],
-        out_specs=[VMEM, VMEM],
-        out_shape=[f32(64, 64), f32(16, LANES)],
-        scratch_shapes=[pltpu.VMEM((72, LANES), jnp.float32)],
-        compiler_params=room(8),
-        cost_estimate=pl.CostEstimate(flops=10**8, bytes_accessed=900_000, transcendentals=0),
-        name="mass",
-    )(basis, classes, level_density)
     local = pl.pallas_call(
         gram_kernel,
-        in_specs=[VMEM] * 3,
+        in_specs=[VMEM] * 3 + [SMEM],
         out_specs=VMEM,
         out_shape=f32(16, 40, LANES),
-        compiler_params=room(8),
+        scratch_shapes=[pltpu.VMEM((72, LANES), jnp.float32)],
+        compiler_params=room(12),
         name="grams",
-    )(basis, image, mass)
+    )(basis, image, classes, level_density)
     gram = total_sum(local)
     residual_pieces, ritz_matrix = pl.pallas_call(
         functools.partial(residual_kernel, total_dofs),
-        in_specs=[VMEM] * 4,
+        in_specs=[VMEM] * 4 + [SMEM],
         out_specs=[VMEM, VMEM],
         out_shape=[f32(1728, LANES), f32(64, 64)],
+        scratch_shapes=[pltpu.VMEM((72, LANES), jnp.float32)],
         compiler_params=room(12),
         name="residual",
-    )(gram, basis, image, band_density)
+    )(gram, basis, image, classes, level_density)
     joined = pl.pallas_call(
         join_kernel,
         in_specs=[VMEM],

time: 107 us -> 104 us (0.972)
  blocking collectives: 48.9 us -> 65.3 us
  waiting for transfers between devices: 18.2 us -> 7.45 us
  starting transfers between devices: 18.9 us -> 14.5 us
  Pallas kernels: 17.8 us -> 14.8 us
    all_to_all x1 -> x2, blocking collectives: 17 us -> 37.4 us  [all_to_all(): lax.all_to_all(x, MODES, split_axis=0, concat_axis=0, tiled=True)]
    all_to_all x2 -> x1, waiting for transfers between devices: 15.1 us -> 4.66 us  [all_to_all(): lax.all_to_all(x, MODES, split_axis=0, concat_axis=0, tiled=True)]
    all_to_all x2 -> x1, starting transfers between devices: 11.3 us -> 6.94 us  [all_to_all(): lax.all_to_all(x, MODES, split_axis=0, concat_axis=0, tiled=True)]
    all_to_all x1, blocking collectives: 15 us -> 12 us  [total_sum(): lax.all_to_all(x, layer_axes, split_axis=0, concat_axis=0, tiled=True)]
    pallas_call x2 -> x1, Pallas kernels: 3.66 us -> 1.79 us  [per_device(): pl.pallas_call(gram_kernel, in_specs=[VMEM] * 3 + [SMEM], out_specs=VMEM,...]
  transfers between devices with their start and end apart: 6 -> 5, of which waited for: 4 -> 3; matrix products, arithmetic and copies ran while one was open for 0% -> 0% of each run, Pallas kernels for 10% -> 8%
where the time goes in v3:
time: 104 us; the launch traced here: 103 us
  blocking collectives  65.3 us (63%)
  Pallas kernels  14.8 us (14%)
  starting transfers between devices  14.5 us (14%)
  waiting for transfers between devices  7.45 us (7%)
    all_to_all x2, blocking collectives, all_to_all(): lax.all_to_all(x, MODES, split_axis=0, concat_axis=0, tiled=True)  37.4 us
    all_to_all x1, blocking collectives, total_sum(): lax.all_to_all(x, 'mesh_1', split_axis=0, concat_axis=0, tiled=True)  15.9 us
    all_to_all x1, blocking collectives, total_sum(): lax.all_to_all(x, layer_axes, split_axis=0, concat_axis=0, tiled=True)  12 us
    ppermute x3, starting transfers between devices, shifted(): return lax.ppermute(x, axis, pairs)  7.49 us
    all_to_all x1, starting transfers between devices, all_to_all(): lax.all_to_all(x, MODES, split_axis=0, concat_axis=0, tiled=True)  6.94 us
    pallas_call x1, Pallas kernels, per_device(): pl.pallas_call(stiffness_kernel, in_specs=[VMEM] * 5 + [SMEM], out_specs=...  6.3 us
    all_to_all x1, waiting for transfers between devices, all_to_all(): lax.all_to_all(x, MODES, split_axis=0, concat_axis=0, tiled=True)  4.66 us
    pallas_call x1, Pallas kernels, per_device(): pl.pallas_call(functools.partial(residual_kernel, total_dofs), in_specs=[...  3.3 us
  transfers between devices with their start and end apart: 5, of which 3 were waited for; matrix products, arithmetic and copies ran while one was open for 0% of the time, Pallas kernels for 8%

profile of v3, /device:TPU:32, one launch (start us, length us, event | category | flops | bytes accessed | tf_op | source)
XLA Modules:
  0.0 102.9 jit_solution(15820149201952265967)
XLA Ops:
  0.6 1.9 %collective-permute-start = (f32[1728,128]{1,0:T(8,128)}, f32[1728,128]{1,0:T(8,128)S(1)}, u32[]{:S(2)}, u32[]{:S(2)}) collective-permute-start(f32[1728,128]{1,0:T(8,128)} %bitcast.21), channel_id=1, source_target_pairs={{0,8},{8,16},{16,24},{24,32},{32,40},{40,48},{48,56},{56,64},{64,7... | collective-permute-start | bytes 2654216 | tf_op jit(solution)/shard_map/ppermute | solution.py:30
  2.6 3.6 %collective-permute-start.1 = (f32[1728,128]{1,0:T(8,128)}, f32[1728,128]{1,0:T(8,128)S(1)}, u32[]{:S(2)}, u32[]{:S(2)}) collective-permute-start(f32[1728,128]{1,0:T(8,128)} %bitcast.22), channel_id=1, source_target_pairs={{8,0},{16,8},{24,16},{32,24},{40,32},{48,40},{56,48},{64,56},{72,6... | collective-permute-start | bytes 2654216 | tf_op jit(solution)/shard_map/ppermute | solution.py:30
  6.2 2.3 %split.1 = f32[1728,128]{1,0:T(8,128)} custom-call(f32[8,3,72,128]{3,2,1,0:T(8,128)} %bitcast.23), custom_call_target="tpu_custom_call" | custom-call | flops 100000 | bytes 1800000 | tf_op jit(solution)/shard_map/split/pallas_call | solution.py:462
  8.6 0.0 copy-start
  8.6 6.9 %all-to-all-start = ((f32[8,216,128]{2,1,0:T(8,128)}), f32[8,216,128]{2,1,0:T(8,128)S(1)}, u32[]{:S(2)}, u32[]{:S(2)}) async-start(f32[8,216,128]{2,1,0:T(8,128)} %bitcast.1), calls=%async_computation | async-start | bytes 1769472 | tf_op jit(solution)/shard_map/all_to_all | solution.py:466
  15.5 0.0 copy-start.2
  15.5 0.0 copy-done
  15.5 1.9 %collective-permute-start.2 = (s32[72,128]{1,0:T(8,128)S(1)}, s32[72,128]{1,0:T(8,128)S(1)}, u32[]{:S(2)}, u32[]{:S(2)}) collective-permute-start(s32[72,128]{1,0:T(8,128)S(1)} %bitcast.18), channel_id=1, source_target_pairs={{8,0},{16,8},{24,16},{32,24},{40,32},{48,40},{56,48},{64,56},{72,6... | collective-permute-start | bytes 110600 | tf_op jit(solution)/shard_map/ppermute | solution.py:30
  17.5 1.6 %collective-permute-done.2.classes_up = s32[72,128]{1,0:T(8,128)S(1)} collective-permute-done((s32[72,128]{1,0:T(8,128)S(1)}, s32[72,128]{1,0:T(8,128)S(1)}, u32[]{:S(2)}, u32[]{:S(2)}) %collective-permute-start.2) | collective-permute-done | bytes 36896 | tf_op jit(solution)/shard_map/ppermute | solution.py:30
  19.1 0.0 collective-permute-done.below
  19.1 0.0 collective-permute-done.1.above
  19.1 0.0 copy-done.2
  19.1 6.3 %stiffness.1 = f32[1728,128]{1,0:T(8,128)S(1)} custom-call(f32[1728,128]{1,0:T(8,128)} %bitcast.24, f32[1728,128]{1,0:T(8,128)S(1)} %collective-permute-done.below, f32[1728,128]{1,0:T(8,128)S(1)} %collective-permute-done.1.above, s32[72,128]{1,0:T(8,128)} %bitcast.17, s32[72,128]{1,0:T(8,128)S(1)} %collective-permute-done.2.classes_up, f32[16]{0:T(128)S(1)} %copy-done.2), custom_call_target="tpu_custom_call" | custom-call | flops 27000000 | bytes 3600000 | tf_op jit(solution)/shard_map/stiffness/pallas_call | solution.py:469
  25.4 4.7 %all-to-all-done = f32[8,216,128]{2,1,0:T(8,128)S(1)} async-done(((f32[8,216,128]{2,1,0:T(8,128)}), f32[8,216,128]{2,1,0:T(8,128)S(1)}, u32[]{:S(2)}, u32[]{:S(2)}) %all-to-all-start) | async-done | bytes 884768 | tf_op jit(solution)/shard_map/all_to_all | solution.py:466
  30.1 20.5 %all_to_all.25 = f32[8,216,128]{2,1,0:T(8,128)S(1)} all-to-all(f32[8,216,128]{2,1,0:T(8,128)S(1)} %bitcast.15), channel_id=1, replica_groups=mesh['mesh_0'=2,'mesh_1'=8,'mesh_2'=2,'modes_0'=2,'modes_1'=4] {'modes_0..., dimensions={0} | all-to-all | bytes 1769472 | tf_op jit(solution)/shard_map/all_to_all | solution.py:466
  50.5 0.0 copy-done.1
  50.5 1.8 %grams.1 = f32[16,40,128]{2,1,0:T(8,128)S(1)} custom-call(f32[1728,128]{1,0:T(8,128)S(1)} %bitcast.10, f32[1728,128]{1,0:T(8,128)S(1)} %bitcast.12, s32[72,128]{1,0:T(8,128)S(1)} %bitcast.19, f32[16]{0:T(128)S(1)} %copy-done.2), custom_call_target="tpu_custom_call" | custom-call | tf_op jit(solution)/shard_map/grams/pallas_call | solution.py:490
  52.3 12.0 %all_to_all.26 = f32[16,40,128]{2,1,0:T(8,128)S(1)} all-to-all(f32[16,40,128]{2,1,0:T(8,128)S(1)} %grams.1), channel_id=1, replica_groups=mesh['mesh_0'=2,'mesh_1'=8,'mesh_2'=2,'modes_0'=2,'modes_1'=4] {'mesh_0'..., dimensions={0} | all-to-all | bytes 655360 | tf_op jit(solution)/shard_map/all_to_all | solution.py:434
  64.3 0.1 collective-permute-start.3
  64.4 1.2 %collective-permute-done.3 = f32[40,128]{1,0:T(8,128)S(1)} collective-permute-done((f32[40,128]{1,0:T(8,128)S(1)}, f32[40,128]{1,0:T(8,128)S(1)}, u32[]{:S(2)}, u32[]{:S(2)}) %collective-permute-start.3) | collective-permute-done | bytes 20512 | tf_op jit(solution)/shard_map/ppermute | solution.py:435
  65.6 15.9 %all_to_all.27 = f32[8,40,128]{2,1,0:T(8,128)S(1)} all-to-all(f32[8,40,128]{2,1,0:T(8,128)S(1)} %broadcast_in_dim.2), channel_id=1, replica_groups=mesh['mesh_0'=2,'mesh_1'=8,'mesh_2'=2,'modes_0'=2,'modes_1'=4] {'mesh_1'}, dimensions={0} | all-to-all | bytes 327680 | tf_op jit(solution)/shard_map/all_to_all | solution.py:437
  81.6 3.3 %residual.1 = (f32[1728,128]{1,0:T(8,128)S(1)}, f32[64,64]{1,0:T(8,128)}) custom-call(f32[40,128]{1,0:T(8,128)S(1)} %reduce_sum.19.gram, f32[1728,128]{1,0:T(8,128)S(1)} %bitcast.11, f32[1728,128]{1,0:T(8,128)S(1)} %bitcast.13, s32[72,128]{1,0:T(8,128)S(1)} %bitcast.20, f32[16]{0:T(128)S(1)} %copy-done.2), custom_call_target="tpu_custom_call" | custom-call | tf_op jit(solution)/shard_map/residual/pallas_call | solution.py:500
  84.9 17.0 %all_to_all.28 = f32[8,216,128]{2,1,0:T(8,128)S(1)} all-to-all(f32[8,216,128]{2,1,0:T(8,128)S(1)} %bitcast.16), channel_id=1, replica_groups=mesh['mesh_0'=2,'mesh_1'=8,'mesh_2'=2,'modes_0'=2,'modes_1'=4] {'modes_0..., dimensions={0} | all-to-all | bytes 1769472 | tf_op jit(solution)/shard_map/all_to_all | solution.py:466
  101.8 1.1 %join.1 = f32[1728,128]{1,0:T(8,128)} custom-call(f32[1728,128]{1,0:T(8,128)S(1)} %bitcast.14), custom_call_target="tpu_custom_call" | custom-call | tf_op jit(solution)/shard_map/join/pallas_call | solution.py:509
  (5 shorter events, 0.1 us)
Async XLA Ops:
  0.6 18.4 %collective-permute-start = (f32[1728,128]{1,0:T(8,128)}, f32[1728,128]{1,0:T(8,128)S(1)}, u32[]{:S(2)}, u32[]{:S(2)}) collective-permute-start(f32[1728,128]{1,0:T(8,128)} %bitcast.21), channel_id=1, source_target_pairs={{0,8},{8,16},{16,24},{24,32},{32,40},{40,48},{48,56},{56,64},{64,7... | collective-permute-start | bytes 2654216 | tf_op jit(solution)/shard_map/ppermute | solution.py:30
  2.6 16.5 %collective-permute-start.1 = (f32[1728,128]{1,0:T(8,128)}, f32[1728,128]{1,0:T(8,128)S(1)}, u32[]{:S(2)}, u32[]{:S(2)}) collective-permute-start(f32[1728,128]{1,0:T(8,128)} %bitcast.22), channel_id=1, source_target_pairs={{8,0},{16,8},{24,16},{32,24},{40,32},{48,40},{56,48},{64,56},{72,6... | collective-permute-start | bytes 2654216 | tf_op jit(solution)/shard_map/ppermute | solution.py:30
  8.6 7.0 %copy-start = (s32[1,9216]{1,0:T(1,128)S(1)}, s32[1,9216]{1,0:T(1,128)}, u32[]{:S(2)}) copy-start(s32[1,9216]{1,0:T(1,128)} %param.4) | copy-start | bytes 110596
  8.6 21.5 %all-to-all-start = ((f32[8,216,128]{2,1,0:T(8,128)}), f32[8,216,128]{2,1,0:T(8,128)S(1)}, u32[]{:S(2)}, u32[]{:S(2)}) async-start(f32[8,216,128]{2,1,0:T(8,128)} %bitcast.1), calls=%async_computation | async-start | bytes 1769472 | tf_op jit(solution)/shard_map/all_to_all | solution.py:466
  15.5 3.6 %copy-start.2 = (f32[16]{0:T(128)S(1)}, f32[16]{0:T(128)}, u32[]{:S(2)}) copy-start(f32[16]{0:T(128)} %levels.5) | copy-start | bytes 196
  15.5 3.5 %collective-permute-start.2 = (s32[72,128]{1,0:T(8,128)S(1)}, s32[72,128]{1,0:T(8,128)S(1)}, u32[]{:S(2)}, u32[]{:S(2)}) collective-permute-start(s32[72,128]{1,0:T(8,128)S(1)} %bitcast.18), channel_id=1, source_target_pairs={{8,0},{16,8},{24,16},{32,24},{40,32},{48,40},{56,48},{64,56},{72,6... | collective-permute-start | bytes 110600 | tf_op jit(solution)/shard_map/ppermute | solution.py:30
  30.0 20.5 %copy-start.1 = (s32[1,9216]{1,0:T(1,128)S(1)}, s32[1,9216]{1,0:T(1,128)}, u32[]{:S(2)}) copy-start(s32[1,9216]{1,0:T(1,128)} %param.4) | copy-start | bytes 110596
  64.3 1.3 %collective-permute-start.3 = (f32[40,128]{1,0:T(8,128)S(1)}, f32[40,128]{1,0:T(8,128)S(1)}, u32[]{:S(2)}, u32[]{:S(2)}) collective-permute-start(f32[40,128]{1,0:T(8,128)S(1)} %reduce_sum.18), channel_id=1, source_target_pairs={{0,8},{8,0},{1,9},{9,1},{2,10},{10,2},{3,11},{11,3},{4,12},{12,4},... | collective-permute-start | bytes 61448 | tf_op jit(solution)/shard_map/ppermute | solution.py:435

commit v4 on v3

--- a/solution.py
+++ b/solution.py
@@ -169,31 +169,31 @@
     before_end = (lane != 95, lane != 63, (lane != 31) & (lane != 127))
     planes = (own, below, above)
 
-    def fetch(h, k):
-        for p in range(3):
-            for c in range(3):
-                u = planes[p][pl.ds(c * 72 + 6 * h + k, 8, stride=216), :]
-                runs[(p * 3 + c) * 6 + k] = u
-                runs[54 + (p * 3 + c) * 6 + k] = pltpu.roll(u, 1, 1)
-
-    def along_x(k):
+    def fetch(h, k, side):
         for s in range(9):
-            u, rolled = runs[s * 6 + k], runs[54 + s * 6 + k]
+            u = planes[s // 3][pl.ds(s % 3 * 72 + 6 * h + k, 8, stride=216), :]
+            runs[side, s * 6 + k] = u
+            runs[side, 54 + s * 6 + k] = pltpu.roll(u, 1, 1)
+
+    def along_x(k, side):
+        for s in range(9):
+            u, rolled = runs[side, s * 6 + k], runs[side, 54 + s * 6 + k]
             back = jnp.where(inside[k % 3], rolled, 0.0)
             if k % 3:
-                back = jnp.where(lane == 0, runs[54 + s * 6 + k - 1], back)
+                back = jnp.where(lane == 0, runs[side, 54 + s * 6 + k - 1], back)
             for n, v in enumerate((u + back, u - back)):
-                x_fields[n * 63 + s * 7 + k + 1] = v
-                turned[n * 63 + s * 7 + k + 1] = pltpu.roll(v, 96, 1)
-
-    def element_forces(h, k):
+                x_fields[side, n * 54 + s * 6 + k] = v
+                turned[side, n * 54 + s * 6 + k] = pltpu.roll(v, 96, 1)
+
+    def element_forces(h, k, side):
         own_f, below_f, above_f = {}, {}, {}
         for p, group in enumerate((own_f, below_f, above_f)):
             for c in range(3):
                 for n, name in enumerate("01"):
-                    at = n * 63 + (p * 3 + c) * 7 + k
-                    row = jnp.where(lane < 96, turned[at], turned[at + 1])
-                    here = x_fields[at + 1]
+                    at = n * 54 + (p * 3 + c) * 6 + k
+                    last = turned[side, at - 1] if k else turned[1 - side, at + 5]
+                    row = jnp.where(lane < 96, last, turned[side, at])
+                    here = x_fields[side, at]
                     group[c, name + "0"] = here + row
                     group[c, name + "1"] = here - row
         even, odd = layer(own_f, below_f)
@@ -207,66 +207,65 @@
                     even_up[c, n] - odd_up[c, n]
                 )
             base = k * 12 + c * 4
-            forces[base] = f["00"] + f["10"]
-            forces[base + 1] = f["01"] + f["11"]
-            forces[base + 2] = pltpu.roll(f["00"] - f["10"], 127, 1)
-            forces[base + 3] = pltpu.roll(f["01"] - f["11"], 127, 1)
-        if k == 5:
-            for at in range(0, 126, 7):
-                turned[at] = turned[at + 6]
-
-    def gather_x(k):
+            forces[side, base] = f["00"] + f["10"]
+            forces[side, base + 1] = f["01"] + f["11"]
+            forces[side, base + 2] = pltpu.roll(f["00"] - f["10"], 127, 1)
+            forces[side, base + 3] = pltpu.roll(f["01"] - f["11"], 127, 1)
+
+    def gather_x(k, side):
         for c in range(3):
             pair = []
             for y in range(2):
                 base = k * 12 + c * 4 + y
-                from_right = jnp.where(before_end[k % 3], forces[base + 2], 0.0)
+                from_right = jnp.where(before_end[k % 3], forces[side, base + 2], 0.0)
                 if k % 3 < 2:
-                    from_right = jnp.where(lane == 127, forces[base + 14], from_right)
-                pair.append(forces[base] + from_right)
-            sums[c * 7 + k + 1] = pair[0] + pair[1]
-            sums[21 + c * 7 + k + 1] = pltpu.roll(pair[0] - pair[1], 32, 1)
-
-    def gather_y(h, k):
+                    from_right = jnp.where(lane == 127, forces[side, base + 14], from_right)
+                pair.append(forces[side, base] + from_right)
+            sums[side, c * 6 + k] = pair[0] + pair[1]
+            sums[side, 18 + c * 6 + k] = pltpu.roll(pair[0] - pair[1], 32, 1)
+
+    def gather_y(h, k, side):
         run = jnp.maximum(6 * h + k - 1, 0)
         row = lax.div(run, 9) * 216 + lax.rem(run, 9)
         for c in range(3):
-            at = c * 7 + k
-            turned_back = jnp.where(lane < 32, sums[21 + at], sums[22 + at])
-            out[pl.ds(row + c * 9, 8, stride=27), :] = sums[at] + turned_back
-        if k == 5:
-            for at in range(0, 42, 7):
-                sums[at] = sums[at + 6]
+            at = c * 6 + k
+            old_side, old = (side, at - 1) if k else (1 - side, at + 5)
+            turned_back = jnp.where(lane < 32, sums[old_side, 18 + old], sums[side, 18 + at])
+            out[pl.ds(row + c * 9, 8, stride=27), :] = sums[old_side, old] + turned_back
 
     zero = jnp.zeros((8, LANES), jnp.float32)
-    for at in range(0, 126, 7):
-        turned[at] = zero
-    for at in range(0, 42, 7):
-        sums[at] = zero
-
-    def step(t, carry=None):
-        fixed = isinstance(t, int)
+    for s in range(18):
+        turned[1, s * 6 + 5] = zero
+    for s in range(6):
+        sums[1, s * 6 + 5] = zero
+
+    def step(t, parity, fixed=True):
+        same, other = parity, 1 - parity
         stages = (
-            (0, 4, 16, lambda k: gather_y(t - 4, k)),
-            (1, 3, 15, gather_x),
-            (1, 2, 14, lambda k: element_forces(t - 2, k)),
-            (2, 1, 13, along_x),
-            (3, 0, 12, lambda k: fetch(t, k)),
+            (4, 16, lambda k: gather_y(t - 4, k, same)),
+            (3, 15, lambda k: gather_x(k, other)),
+            (2, 14, lambda k: element_forces(t - 2, k, same)),
+            (1, 13, lambda k: along_x(k, other)),
+            (0, 12, lambda k: fetch(t, k, same)),
         )
-        for turn in range(9):
-            for delay, start, end, stage in stages:
-                if 0 <= turn - delay < 6 and (not fixed or start <= t < end):
-                    stage(turn - delay)
+        for k in range(6):
+            for start, end, stage in stages:
+                if not fixed or start <= t < end:
+                    stage(k)
+
+    def two_steps(i, carry):
+        step(2 * i, 0, False)
+        step(2 * i + 1, 1, False)
         return carry
 
     for t in range(4):
-        step(t)
-    lax.fori_loop(4, 12, step, 0)
+        step(t, t % 2)
+    lax.fori_loop(2, 6, two_steps, 0)
     for t in range(12, 16):
-        step(t)
+        step(t, t % 2)
     for c in range(3):
-        out[pl.ds(7 * 216 + 8 + c * 9, 8, stride=27), :] = sums[c * 7] + jnp.where(
-            lane < 32, sums[21 + c * 7], 0.0
+        out[pl.ds(7 * 216 + 8 + c * 9, 8, stride=27), :] = sums[1, c * 6 + 5] + jnp.where(
+            lane < 32, sums[1, 18 + c * 6 + 5], 0.0
         )
 
 
@@ -472,7 +471,7 @@
         out_specs=VMEM,
         out_shape=f32(1728, LANES),
         scratch_shapes=[pltpu.VMEM((72, LANES), jnp.float32)] * 2
-        + [pltpu.VMEM((n, 8, LANES), jnp.float32) for n in (108, 126, 126, 72, 42)],
+        + [pltpu.VMEM((2, n, 8, LANES), jnp.float32) for n in (108, 108, 108, 72, 36)],
         compiler_params=room(12),
         cost_estimate=pl.CostEstimate(
             flops=27_000_000, bytes_accessed=3_600_000, transcendentals=0

time: 104 us -> 104 us (level)
  no operation moved by 1% of the time
where the time goes in v4:
time: 104 us; the launch traced here: 103 us
  blocking collectives  65.3 us (63%)
  starting transfers between devices  14.5 us (14%)
  Pallas kernels  14.2 us (14%)
  waiting for transfers between devices  8.03 us (8%)
    all_to_all x2, blocking collectives, all_to_all(): lax.all_to_all(x, MODES, split_axis=0, concat_axis=0, tiled=True)  36.8 us
    all_to_all x1, blocking collectives, total_sum(): lax.all_to_all(x, 'mesh_1', split_axis=0, concat_axis=0, tiled=True)  16.8 us
    all_to_all x1, blocking collectives, total_sum(): lax.all_to_all(x, layer_axes, split_axis=0, concat_axis=0, tiled=True)  11.7 us
    ppermute x3, starting transfers between devices, shifted(): return lax.ppermute(x, axis, pairs)  7.49 us
    all_to_all x1, starting transfers between devices, all_to_all(): lax.all_to_all(x, MODES, split_axis=0, concat_axis=0, tiled=True)  6.94 us
    pallas_call x1, Pallas kernels, per_device(): pl.pallas_call(stiffness_kernel, in_specs=[VMEM] * 5 + [SMEM], out_specs=...  5.73 us
    all_to_all x1, waiting for transfers between devices, all_to_all(): lax.all_to_all(x, MODES, split_axis=0, concat_axis=0, tiled=True)  5.23 us
    pallas_call x1, Pallas kernels, per_device(): pl.pallas_call(functools.partial(residual_kernel, total_dofs), in_specs=[...  3.3 us
  transfers between devices with their start and end apart: 5, of which 3 were waited for; matrix products, arithmetic and copies ran while one was open for 0% of the time, Pallas kernels for 8%

profile of v4, /device:TPU:32, one launch (start us, length us, event | category | flops | bytes accessed | tf_op | source)
XLA Modules:
  0.0 102.9 jit_solution(1404415429117862747)
XLA Ops:
  0.6 1.9 %collective-permute-start = (f32[1728,128]{1,0:T(8,128)}, f32[1728,128]{1,0:T(8,128)S(1)}, u32[]{:S(2)}, u32[]{:S(2)}) collective-permute-start(f32[1728,128]{1,0:T(8,128)} %bitcast.21), channel_id=1, source_target_pairs={{0,8},{8,16},{16,24},{24,32},{32,40},{40,48},{48,56},{56,64},{64,7... | collective-permute-start | bytes 2654216 | tf_op jit(solution)/shard_map/ppermute | solution.py:30
  2.6 3.6 %collective-permute-start.1 = (f32[1728,128]{1,0:T(8,128)}, f32[1728,128]{1,0:T(8,128)S(1)}, u32[]{:S(2)}, u32[]{:S(2)}) collective-permute-start(f32[1728,128]{1,0:T(8,128)} %bitcast.22), channel_id=1, source_target_pairs={{8,0},{16,8},{24,16},{32,24},{40,32},{48,40},{56,48},{64,56},{72,6... | collective-permute-start | bytes 2654216 | tf_op jit(solution)/shard_map/ppermute | solution.py:30
  6.2 2.3 %split.1 = f32[1728,128]{1,0:T(8,128)} custom-call(f32[8,3,72,128]{3,2,1,0:T(8,128)} %bitcast.23), custom_call_target="tpu_custom_call" | custom-call | flops 100000 | bytes 1800000 | tf_op jit(solution)/shard_map/split/pallas_call | solution.py:461
  8.6 0.0 copy-start
  8.6 6.9 %all-to-all-start = ((f32[8,216,128]{2,1,0:T(8,128)}), f32[8,216,128]{2,1,0:T(8,128)S(1)}, u32[]{:S(2)}, u32[]{:S(2)}) async-start(f32[8,216,128]{2,1,0:T(8,128)} %bitcast.1), calls=%async_computation | async-start | bytes 1769472 | tf_op jit(solution)/shard_map/all_to_all | solution.py:465
  15.5 0.0 copy-start.2
  15.5 0.0 copy-done
  15.5 1.9 %collective-permute-start.2 = (s32[72,128]{1,0:T(8,128)S(1)}, s32[72,128]{1,0:T(8,128)S(1)}, u32[]{:S(2)}, u32[]{:S(2)}) collective-permute-start(s32[72,128]{1,0:T(8,128)S(1)} %bitcast.18), channel_id=1, source_target_pairs={{8,0},{16,8},{24,16},{32,24},{40,32},{48,40},{56,48},{64,56},{72,6... | collective-permute-start | bytes 110600 | tf_op jit(solution)/shard_map/ppermute | solution.py:30
  17.5 1.6 %collective-permute-done.2.classes_up = s32[72,128]{1,0:T(8,128)S(1)} collective-permute-done((s32[72,128]{1,0:T(8,128)S(1)}, s32[72,128]{1,0:T(8,128)S(1)}, u32[]{:S(2)}, u32[]{:S(2)}) %collective-permute-start.2) | collective-permute-done | bytes 36896 | tf_op jit(solution)/shard_map/ppermute | solution.py:30
  19.1 0.0 collective-permute-done.below
  19.1 0.0 collective-permute-done.1.above
  19.1 0.0 copy-done.2
  19.1 5.7 %stiffness.1 = f32[1728,128]{1,0:T(8,128)S(1)} custom-call(f32[1728,128]{1,0:T(8,128)} %bitcast.24, f32[1728,128]{1,0:T(8,128)S(1)} %collective-permute-done.below, f32[1728,128]{1,0:T(8,128)S(1)} %collective-permute-done.1.above, s32[72,128]{1,0:T(8,128)} %bitcast.17, s32[72,128]{1,0:T(8,128)S(1)} %collective-permute-done.2.classes_up, f32[16]{0:T(128)S(1)} %copy-done.2), custom_call_target="tpu_custom_call" | custom-call | flops 27000000 | bytes 3600000 | tf_op jit(solution)/shard_map/stiffness/pallas_call | solution.py:468
  24.8 5.2 %all-to-all-done = f32[8,216,128]{2,1,0:T(8,128)S(1)} async-done(((f32[8,216,128]{2,1,0:T(8,128)}), f32[8,216,128]{2,1,0:T(8,128)S(1)}, u32[]{:S(2)}, u32[]{:S(2)}) %all-to-all-start) | async-done | bytes 884768 | tf_op jit(solution)/shard_map/all_to_all | solution.py:465
  30.1 19.9 %all_to_all.25 = f32[8,216,128]{2,1,0:T(8,128)S(1)} all-to-all(f32[8,216,128]{2,1,0:T(8,128)S(1)} %bitcast.15), channel_id=1, replica_groups=mesh['mesh_0'=2,'mesh_1'=8,'mesh_2'=2,'modes_0'=2,'modes_1'=4] {'modes_0..., dimensions={0} | all-to-all | bytes 1769472 | tf_op jit(solution)/shard_map/all_to_all | solution.py:465
  49.9 0.0 copy-done.1
  49.9 1.8 %grams.1 = f32[16,40,128]{2,1,0:T(8,128)S(1)} custom-call(f32[1728,128]{1,0:T(8,128)S(1)} %bitcast.10, f32[1728,128]{1,0:T(8,128)S(1)} %bitcast.12, s32[72,128]{1,0:T(8,128)S(1)} %bitcast.19, f32[16]{0:T(128)S(1)} %copy-done.2), custom_call_target="tpu_custom_call" | custom-call | tf_op jit(solution)/shard_map/grams/pallas_call | solution.py:489
  51.7 11.7 %all_to_all.26 = f32[16,40,128]{2,1,0:T(8,128)S(1)} all-to-all(f32[16,40,128]{2,1,0:T(8,128)S(1)} %grams.1), channel_id=1, replica_groups=mesh['mesh_0'=2,'mesh_1'=8,'mesh_2'=2,'modes_0'=2,'modes_1'=4] {'mesh_0'..., dimensions={0} | all-to-all | bytes 655360 | tf_op jit(solution)/shard_map/all_to_all | solution.py:433
  63.4 0.1 collective-permute-start.3
  63.5 1.2 %collective-permute-done.3 = f32[40,128]{1,0:T(8,128)S(1)} collective-permute-done((f32[40,128]{1,0:T(8,128)S(1)}, f32[40,128]{1,0:T(8,128)S(1)}, u32[]{:S(2)}, u32[]{:S(2)}) %collective-permute-start.3) | collective-permute-done | bytes 20512 | tf_op jit(solution)/shard_map/ppermute | solution.py:434
  64.7 16.8 %all_to_all.27 = f32[8,40,128]{2,1,0:T(8,128)S(1)} all-to-all(f32[8,40,128]{2,1,0:T(8,128)S(1)} %broadcast_in_dim.2), channel_id=1, replica_groups=mesh['mesh_0'=2,'mesh_1'=8,'mesh_2'=2,'modes_0'=2,'modes_1'=4] {'mesh_1'}, dimensions={0} | all-to-all | bytes 327680 | tf_op jit(solution)/shard_map/all_to_all | solution.py:436
  81.6 3.3 %residual.1 = (f32[1728,128]{1,0:T(8,128)S(1)}, f32[64,64]{1,0:T(8,128)}) custom-call(f32[40,128]{1,0:T(8,128)S(1)} %reduce_sum.19.gram, f32[1728,128]{1,0:T(8,128)S(1)} %bitcast.11, f32[1728,128]{1,0:T(8,128)S(1)} %bitcast.13, s32[72,128]{1,0:T(8,128)S(1)} %bitcast.20, f32[16]{0:T(128)S(1)} %copy-done.2), custom_call_target="tpu_custom_call" | custom-call | tf_op jit(solution)/shard_map/residual/pallas_call | solution.py:499
  84.9 17.0 %all_to_all.28 = f32[8,216,128]{2,1,0:T(8,128)S(1)} all-to-all(f32[8,216,128]{2,1,0:T(8,128)S(1)} %bitcast.16), channel_id=1, replica_groups=mesh['mesh_0'=2,'mesh_1'=8,'mesh_2'=2,'modes_0'=2,'modes_1'=4] {'modes_0..., dimensions={0} | all-to-all | bytes 1769472 | tf_op jit(solution)/shard_map/all_to_all | solution.py:465
  101.8 1.1 %join.1 = f32[1728,128]{1,0:T(8,128)} custom-call(f32[1728,128]{1,0:T(8,128)S(1)} %bitcast.14), custom_call_target="tpu_custom_call" | custom-call | tf_op jit(solution)/shard_map/join/pallas_call | solution.py:508
  (5 shorter events, 0.1 us)
Async XLA Ops:
  0.6 18.4 %collective-permute-start = (f32[1728,128]{1,0:T(8,128)}, f32[1728,128]{1,0:T(8,128)S(1)}, u32[]{:S(2)}, u32[]{:S(2)}) collective-permute-start(f32[1728,128]{1,0:T(8,128)} %bitcast.21), channel_id=1, source_target_pairs={{0,8},{8,16},{16,24},{24,32},{32,40},{40,48},{48,56},{56,64},{64,7... | collective-permute-start | bytes 2654216 | tf_op jit(solution)/shard_map/ppermute | solution.py:30
  2.6 16.5 %collective-permute-start.1 = (f32[1728,128]{1,0:T(8,128)}, f32[1728,128]{1,0:T(8,128)S(1)}, u32[]{:S(2)}, u32[]{:S(2)}) collective-permute-start(f32[1728,128]{1,0:T(8,128)} %bitcast.22), channel_id=1, source_target_pairs={{8,0},{16,8},{24,16},{32,24},{40,32},{48,40},{56,48},{64,56},{72,6... | collective-permute-start | bytes 2654216 | tf_op jit(solution)/shard_map/ppermute | solution.py:30
  8.6 7.0 %copy-start = (s32[1,9216]{1,0:T(1,128)S(1)}, s32[1,9216]{1,0:T(1,128)}, u32[]{:S(2)}) copy-start(s32[1,9216]{1,0:T(1,128)} %param.4) | copy-start | bytes 110596
  8.6 21.5 %all-to-all-start = ((f32[8,216,128]{2,1,0:T(8,128)}), f32[8,216,128]{2,1,0:T(8,128)S(1)}, u32[]{:S(2)}, u32[]{:S(2)}) async-start(f32[8,216,128]{2,1,0:T(8,128)} %bitcast.1), calls=%async_computation | async-start | bytes 1769472 | tf_op jit(solution)/shard_map/all_to_all | solution.py:465
  15.5 3.6 %copy-start.2 = (f32[16]{0:T(128)S(1)}, f32[16]{0:T(128)}, u32[]{:S(2)}) copy-start(f32[16]{0:T(128)} %levels.5) | copy-start | bytes 196
  15.5 3.5 %collective-permute-start.2 = (s32[72,128]{1,0:T(8,128)S(1)}, s32[72,128]{1,0:T(8,128)S(1)}, u32[]{:S(2)}, u32[]{:S(2)}) collective-permute-start(s32[72,128]{1,0:T(8,128)S(1)} %bitcast.18), channel_id=1, source_target_pairs={{8,0},{16,8},{24,16},{32,24},{40,32},{48,40},{56,48},{64,56},{72,6... | collective-permute-start | bytes 110600 | tf_op jit(solution)/shard_map/ppermute | solution.py:30
  30.0 19.9 %copy-start.1 = (s32[1,9216]{1,0:T(1,128)S(1)}, s32[1,9216]{1,0:T(1,128)}, u32[]{:S(2)}) copy-start(s32[1,9216]{1,0:T(1,128)} %param.4) | copy-start | bytes 110596
  63.4 1.3 %collective-permute-start.3 = (f32[40,128]{1,0:T(8,128)S(1)}, f32[40,128]{1,0:T(8,128)S(1)}, u32[]{:S(2)}, u32[]{:S(2)}) collective-permute-start(f32[40,128]{1,0:T(8,128)S(1)} %reduce_sum.18), channel_id=1, source_target_pairs={{0,8},{8,0},{1,9},{9,1},{2,10},{10,2},{3,11},{11,3},{4,12},{12,4},... | collective-permute-start | bytes 61448 | tf_op jit(solution)/shard_map/ppermute | solution.py:434
